TPU v7x, 32 devices: a whole 2x2x4 slice. The times are simulated.
32 devices in a mesh: fsdp: 8 (over y, x, core), tensor: 4 (over z).
Axes of the slice: x: 2, y: 2, z: 4, core: 2. Of those that a mesh axis runs over, the one named last changes fastest.
Arguments:
- inputs: bfloat16 [32, 577, 1024], P('fsdp'), may hold values from -6 to 6
- lengths: int32 [32], P('fsdp'), may hold values from 144 to 577, as said below
- norm_gains: bfloat16 [2, 1024], P(None, 'fsdp'), may hold values from 0.5 to 1.5
- norm_shifts: bfloat16 [2, 1024], P(None, 'fsdp'), may hold values from -1.5 to 1.5
- w_qkv: bfloat16 [3, 1024, 1024], P(None, 'fsdp', 'tensor'), may hold values from -0.1875 to 0.1875
- bias_qv: bfloat16 [2, 1024], P(None, 'tensor'), may hold values from -3 to 3
- w_out: bfloat16 [1024, 1024], P('tensor', 'fsdp'), may hold values from -1.5 to 1.5
- out_bias: bfloat16 [2, 1024], P(None, 'fsdp'), may hold values from -1.5 to 1.5
- w_up: bfloat16 [1024, 4096], P('fsdp', 'tensor'), may hold values from -0.1875 to 0.1875
- b_up: bfloat16 [4096], P('tensor'), may hold values from -3 to 3
- w_down: bfloat16 [4096, 1024], P('tensor', 'fsdp'), may hold values from -0.375 to 0.375
- cotangent: bfloat16 [32, 577, 1024], P('fsdp'), may hold values from -6 to 6
Outputs:
- output: bfloat16 [32, 577, 1024], P('fsdp')
- grad_input: float32 [32, 577, 1024], P('fsdp')
- grad_gains: float32 [2, 1024], P(None, 'fsdp')
- grad_shifts: float32 [2, 1024], P(None, 'fsdp')
- grad_qkv: float32 [3, 1024, 1024], P(None, 'fsdp', 'tensor')
- grad_bias_qv: float32 [2, 1024], P(None, 'tensor')
- grad_out: float32 [1024, 1024], P('tensor', 'fsdp')
- grad_out_bias: float32 [2, 1024], P(None, 'fsdp')
- grad_up: float32 [1024, 4096], P('fsdp', 'tensor')
- grad_b_up: float32 [4096], P('tensor')
- grad_down: float32 [4096, 1024], P('tensor', 'fsdp')
Inputs may be any that keep to these rules, and one draw needn't show every extreme that they name: lengths[b] counts the valid leading tokens of image b; some image has all 577 valid and some has 144.
All inputs are finite; a program needn't handle non-finite values.
Results may differ from a plain program's by a relative error of at most 0.02.
Values may be sent and summed in bfloat16 or wider, within the bound.
A program may use at most 256 MiB of HBM per device.

v0:
```python
import jax
import jax.numpy as jnp
from jax import lax
from jax.sharding import PartitionSpec as P

HEAD = 64


epsilon = 1e-06
half_root = 0.7071067811865476
density_scale = 0.3989422804014327


def normalize(tokens):
    average = jnp.mean(tokens, axis=-1, keepdims=True)
    centred = tokens - average
    spread = jnp.mean(centred * centred, axis=-1, keepdims=True)
    inverse = lax.rsqrt(spread + epsilon)
    return (centred * inverse, inverse)


def normalize_back(incoming, normed, inverse, gain):
    scaled = incoming * gain
    return inverse * (
        scaled
        - jnp.mean(scaled, axis=-1, keepdims=True)
        - normed * jnp.mean(scaled * normed, axis=-1, keepdims=True)
    )


def masked_scores(query_heads, key_heads, valid, scale):
    scores = (
        jnp.einsum("bqhe,bkhe->bhqk", query_heads, key_heads, preferred_element_type=jnp.float32)
        * scale
    )
    return jnp.where(valid[:, None, None, :], scores, -jnp.inf)


def local(
    inputs,
    lengths,
    norm_gains,
    norm_shifts,
    w_qkv,
    bias_qv,
    w_out,
    out_bias,
    w_up,
    b_up,
    w_down,
    cotangent,
):
    batch, seq_len, width = inputs.shape
    tokens = batch * seq_len
    local_width = w_qkv.shape[2]
    local_heads = local_width // HEAD
    scale = HEAD ** (-0.5)
    gathered = (
        lax.all_gather(w_qkv, "fsdp", axis=1, tiled=True),
        lax.all_gather(w_out, "fsdp", axis=1, tiled=True),
        lax.all_gather(w_up, "fsdp", axis=0, tiled=True),
        lax.all_gather(w_down, "fsdp", axis=1, tiled=True),
        lax.all_gather(norm_gains, "fsdp", axis=1, tiled=True),
        lax.all_gather(norm_shifts, "fsdp", axis=1, tiled=True),
        lax.all_gather(out_bias, "fsdp", axis=1, tiled=True),
    )
    full_qkv, full_out, full_up, full_down, all_gains, all_shifts, all_bias = gathered
    gain_rows = all_gains.astype(jnp.float32)
    shift_rows = all_shifts.astype(jnp.float32)
    bias_rows = all_bias.astype(jnp.float32)
    proj_bias = bias_qv.astype(jnp.float32)
    hidden_bias = b_up.astype(jnp.float32)
    flat_in = inputs.reshape(tokens, width).astype(jnp.float32)
    normed_one, inverse_one = normalize(flat_in)
    hidden_one = (normed_one * gain_rows[0] + shift_rows[0]).astype(jnp.bfloat16)
    projected = jnp.einsum("rd,cde->cre", hidden_one, full_qkv, preferred_element_type=jnp.float32)
    queries = (projected[0] + proj_bias[0]).astype(jnp.bfloat16)
    key_rows = projected[1].astype(jnp.bfloat16)
    value_rows = (projected[2] + proj_bias[1]).astype(jnp.bfloat16)
    head_shape = (batch, seq_len, local_heads, HEAD)
    query_heads = queries.reshape(head_shape)
    key_heads = key_rows.reshape(head_shape)
    value_heads = value_rows.reshape(head_shape)
    valid = lax.broadcasted_iota(jnp.int32, (batch, seq_len), 1) < lengths[:, None]
    scores = masked_scores(query_heads, key_heads, valid, scale)
    top = jnp.max(scores, axis=-1, keepdims=True)
    log_total = top + jnp.log(jnp.sum(jnp.exp(scores - top), axis=-1, keepdims=True))
    weights_b = jnp.exp(scores - log_total).astype(jnp.bfloat16)
    attended_heads = jnp.einsum(
        "bhqk,bkhe->bqhe", weights_b, value_heads, preferred_element_type=jnp.float32
    ).astype(jnp.bfloat16)
    attended = attended_heads.reshape(tokens, local_width)
    attn_total = lax.psum(
        jnp.dot(attended, full_out, preferred_element_type=jnp.float32).astype(jnp.bfloat16),
        "tensor",
    ).astype(jnp.float32)
    middle = flat_in + (attn_total + bias_rows[0])
    normed_two, inverse_two = normalize(middle)
    hidden_two = (normed_two * gain_rows[1] + shift_rows[1]).astype(jnp.bfloat16)
    before = jnp.dot(hidden_two, full_up, preferred_element_type=jnp.float32) + hidden_bias
    activated = jax.nn.gelu(before, approximate=False).astype(jnp.bfloat16)
    mlp_total = lax.psum(
        jnp.dot(activated, full_down, preferred_element_type=jnp.float32).astype(jnp.bfloat16),
        "tensor",
    ).astype(jnp.float32)
    result = (middle + (mlp_total + bias_rows[1])).astype(jnp.bfloat16)
    back_qkv, back_out, back_up, back_down = (full_qkv, full_out, full_up, full_down)
    grad_rows = cotangent.reshape(tokens, width)
    grad_f = grad_rows.astype(jnp.float32)
    grad_down = jnp.einsum("rf,rd->fd", activated, grad_rows, preferred_element_type=jnp.float32)
    dact = jnp.einsum("rd,fd->rf", grad_rows, back_down, preferred_element_type=jnp.float32)
    normal_cdf = 0.5 * (1.0 + jax.scipy.special.erf(before * half_root))
    density = jnp.exp(-0.5 * before * before) * density_scale
    dbefore = dact * (normal_cdf + before * density)
    dbefore_b = dbefore.astype(jnp.bfloat16)
    grad_b_up = jnp.sum(dbefore, axis=0)
    grad_up = jnp.einsum("rd,rf->df", hidden_two, dbefore_b, preferred_element_type=jnp.float32)
    dhidden_two = lax.psum(
        jnp.einsum("rf,df->rd", dbefore_b, back_up, preferred_element_type=jnp.float32).astype(
            jnp.bfloat16
        ),
        "tensor",
    ).astype(jnp.float32)
    dmiddle = grad_f + normalize_back(dhidden_two, normed_two, inverse_two, gain_rows[1])
    dmiddle_b = dmiddle.astype(jnp.bfloat16)
    grad_out = jnp.einsum("rk,rd->kd", attended, dmiddle_b, preferred_element_type=jnp.float32)
    grad_out_bias = jnp.stack([jnp.sum(dmiddle, axis=0), jnp.sum(grad_f, axis=0)])
    dattended = jnp.einsum(
        "rd,kd->rk", dmiddle_b, back_out, preferred_element_type=jnp.float32
    ).astype(jnp.bfloat16)
    dattended_heads = dattended.reshape(head_shape)
    again_scores = masked_scores(query_heads, key_heads, valid, scale)
    prob = jnp.exp(again_scores - log_total)
    again_weights = prob.astype(jnp.bfloat16)
    dprob = jnp.einsum(
        "bqhe,bkhe->bhqk", dattended_heads, value_heads, preferred_element_type=jnp.float32
    )
    delta = jnp.einsum(
        "bqhe,bqhe->bhq", dattended_heads, attended_heads, preferred_element_type=jnp.float32
    )[..., None]
    dscores = (prob * (dprob - delta) * scale).astype(jnp.bfloat16)
    dqueries = jnp.einsum(
        "bhqk,bkhe->bqhe", dscores, key_heads, preferred_element_type=jnp.float32
    ).reshape(tokens, local_width)
    dkeys = jnp.einsum(
        "bhqk,bqhe->bkhe", dscores, query_heads, preferred_element_type=jnp.float32
    ).reshape(tokens, local_width)
    dvalues = jnp.einsum(
        "bhqk,bqhe->bkhe", again_weights, dattended_heads, preferred_element_type=jnp.float32
    ).reshape(tokens, local_width)
    grad_bias_part = jnp.stack([jnp.sum(dqueries, axis=0), jnp.sum(dvalues, axis=0)])
    stacked = jnp.stack([dqueries, dkeys, dvalues]).astype(jnp.bfloat16)
    grad_qkv = jnp.einsum("rd,cre->cde", hidden_one, stacked, preferred_element_type=jnp.float32)
    dhidden_one = lax.psum(
        jnp.einsum("cre,cde->rd", stacked, back_qkv, preferred_element_type=jnp.float32).astype(
            jnp.bfloat16
        ),
        "tensor",
    ).astype(jnp.float32)
    grad_input = dmiddle + normalize_back(dhidden_one, normed_one, inverse_one, gain_rows[0])
    grad_gains = jnp.stack(
        [jnp.sum(dhidden_one * normed_one, axis=0), jnp.sum(dhidden_two * normed_two, axis=0)]
    )
    grad_shifts = jnp.stack([jnp.sum(dhidden_one, axis=0), jnp.sum(dhidden_two, axis=0)])
    owned_qkv, owned_out, owned_up, owned_down, owned_gains, owned_shifts, owned_bias = (
        lax.psum_scatter(
            grad_qkv.astype(jnp.bfloat16), "fsdp", scatter_dimension=1, tiled=True
        ).astype(jnp.float32),
        lax.psum_scatter(
            grad_out.astype(jnp.bfloat16), "fsdp", scatter_dimension=1, tiled=True
        ).astype(jnp.float32),
        lax.psum_scatter(
            grad_up.astype(jnp.bfloat16), "fsdp", scatter_dimension=0, tiled=True
        ).astype(jnp.float32),
        lax.psum_scatter(
            grad_down.astype(jnp.bfloat16), "fsdp", scatter_dimension=1, tiled=True
        ).astype(jnp.float32),
        lax.psum_scatter(
            grad_gains.astype(jnp.bfloat16), "fsdp", scatter_dimension=1, tiled=True
        ).astype(jnp.float32),
        lax.psum_scatter(
            grad_shifts.astype(jnp.bfloat16), "fsdp", scatter_dimension=1, tiled=True
        ).astype(jnp.float32),
        lax.psum_scatter(
            grad_out_bias.astype(jnp.bfloat16), "fsdp", scatter_dimension=1, tiled=True
        ).astype(jnp.float32),
    )
    summed_bias_qv, summed_b_up = lax.psum((grad_bias_part, grad_b_up), "fsdp")
    return (
        result.reshape(batch, seq_len, width),
        grad_input.reshape(batch, seq_len, width),
        owned_gains,
        owned_shifts,
        owned_qkv,
        summed_bias_qv,
        owned_out,
        owned_bias,
        owned_up,
        summed_b_up,
        owned_down,
    )


def solution(mesh):
    placed = (
        P("fsdp", None, None),
        P("fsdp"),
        P(None, "fsdp"),
        P(None, "fsdp"),
        P(None, "fsdp", "tensor"),
        P(None, "tensor"),
        P("tensor", "fsdp"),
        P(None, "fsdp"),
        P("fsdp", "tensor"),
        P("tensor"),
        P("tensor", "fsdp"),
        P("fsdp", None, None),
    )
    return jax.shard_map(
        local,
        mesh=mesh,
        in_specs=placed,
        out_specs=(
            P("fsdp", None, None),
            P("fsdp", None, None),
            P(None, "fsdp"),
            P(None, "fsdp"),
            P(None, "fsdp", "tensor"),
            P(None, "tensor"),
            P("tensor", "fsdp"),
            P(None, "fsdp"),
            P("fsdp", "tensor"),
            P("tensor"),
            P("tensor", "fsdp"),
        ),
        check_vma=False,
    )
```

profile of v0, /device:TPU:0, one launch (start us, length us, event | category | flops | bytes accessed | tf_op | source)
XLA Modules:
  0.0 1187.5 jit_solution(13304505593827600482)
XLA Ops:
  33.3 10.2 all_gather.21
  52.3 9.2 all_gather.24
  98.8 10.7 fusion.1
  109.5 11.2 exponential_reduce_fusion
  120.8 10.8 convolution_convert_fusion.7
  160.9 150.4 %all-reduce.6.cloned.1.call-done = bf16[2308,1024]{1,0:T(8,128)(2,1)} async-done(((bf16[2308,1024]{1,0:T(8,128)(2,1)}), bf16[2308,1024]{1,0:T(8,128)(2,1)}) %all-reduce.6.cloned.1.call-update) | async-done | bytes 4726800 | tf_op jit(solution)/shard_map/psum | solution.py:93
  311.3 10.0 fusion.66
  326.1 13.9 %all-gather.6.cloned.1.call-done = bf16[1024,1024]{1,0:T(8,128)(2,1)} async-done(((bf16[128,1024]{1,0:T(8,128)(2,1)}), bf16[1024,1024]{1,0:T(8,128)(2,1)}) %all-gather.6.cloned.1.call-update) | async-done | bytes 2097168 | tf_op jit(solution)/shard_map/all_gather | solution.py:61
  340.0 30.2 %fusion.20 = (bf16[2308,1024]{1,0:T(8,128)(2,1)}, f32[2308,1024]{1,0:T(8,128)}) fusion(f32[1024]{0:T(1024)S(1)} %convert_element_type.159, bf16[1024,1024]{1,0:T(8,128)(2,1)} %all-gather.6.cloned.1.call-done, f32[2308,1024]{1,0:T(8,128)} %get-tuple-element.70, f32[1024]{0:T(1024)S(1)} %bitcast.111, f32[1024]{0:T(1024)S(1)} %bitcast.100, ...), kind=kOutput, calls=%fused_computation.30 | convolution fusion | flops 5008027648 | bytes 25761824 | tf_op jit(solution)/shard_map/dot_general | solution.py:100
  370.2 12.2 %fusion.71 = (f32[1024]{0:T(1024)}, bf16[2308,1024]{1,0:T(8,128)(2,1)S(1)}) fusion(f32[2308,1024]{1,0:T(8,128)} %get-tuple-element.82, f32[1024]{0:T(1024)S(1)} %convert_element_type.159, bf16[2308,1024]{1,0:T(8,128)(2,1)} %reshape.151, bf16[1024,1024]{1,0:T(8,128)(2,1)} %all-gather.8.cloned.1.call-done), kind=kOutput, calls=%fused_computation.127 | convolution fusion | flops 4868586496 | bytes 21012480 | tf_op jit(solution)/shard_map/rd,fd->rf/dot_general | solution.py:111
  391.4 9.1 convolution_convert_fusion.4
  407.5 13.2 %fusion.40 = bf16[1024,1024]{1,0:T(8,128)(2,1)} fusion(bf16[2308,1024]{1,0:T(8,128)(2,1)} %copy-done.39, f32[2308,1024]{1,0:T(8,128)} %get-tuple-element.70, f32[1024]{0:T(1024)S(1)} %bitcast.112, f32[1024]{0:T(1024)S(1)} %bitcast.101, f32[2308]{0:T(1024)S(1)} %add_rsqrt_fusion.1, f32[2308]{0:T(1024)S(1)} %broadcast_multiply_fusion.5), kind=kOutput, calls=%fused_computation.81 | convolution fusion | flops 4853092352 | bytes 16304160 | tf_op jit(solution)/shard_map/rd,rf->df/dot_general | solution.py:117
  420.8 143.4 %all-reduce.8.cloned.1.call-done = bf16[2308,1024]{1,0:T(8,128)(2,1)} async-done(((bf16[2308,1024]{1,0:T(8,128)(2,1)}), bf16[2308,1024]{1,0:T(8,128)(2,1)}) %all-reduce.8.cloned.1.call-update) | async-done | bytes 4726800 | tf_op jit(solution)/shard_map/psum | solution.py:118
  564.2 9.3 fusion.12
  593.0 17.3 %multiply_convert_fusion = bf16[4,4,577,577]{2,3,1,0:T(8,128)(2,1)} fusion(f32[4,4,577,577]{2,3,1,0:T(8,128)} %get-tuple-element.80, f32[4,4,577]{2,1,0:T(4,128)S(1)} %multiply_reduce_fusion.2, f32[4,4,577]{2,1,0:T(4,128)S(1)} %bitcast.94, pred[4,577]{1,0:T(4,128)(4,1)S(1)} %copy-done.21, bf16[4,577,4,64]{1,0,3,2:T(4,128)(2,1)} %reshape.152, ...), kind=kOutput, calls=%fused_computation | convolution fusion | flops 719126592 | bytes 34400740 | tf_op jit(solution)/shard_map/bqhe,bkhe->bhqk/dot_general | solution.py:135
  627.8 9.6 fusion.44
  637.4 12.3 %bitcast_convert_fusion.1 = (bf16[4,577,4,64]{1,3,2,0:T(8,128)(2,1)}, f32[4,4,64,577]{3,2,1,0:T(8,128)}) fusion(f32[4,4,577,577]{2,3,1,0:T(8,128)} %get-tuple-element.80, f32[4,4,577]{2,1,0:T(4,128)S(1)} %bitcast.95, pred[4,577]{1,0:T(4,128)(4,1)S(1)} %copy-done.21, bf16[4,577,4,64]{1,0,3,2:T(4,128)(2,1)S(1)} %copy-done.11), kind=kOutput, calls=%fused_computation.68 | convolution fusion | flops 703736896 | bytes 26073476 | tf_op jit(solution)/shard_map/bhqk,bqhe->bkhe/dot_general | solution.py:148
  665.6 10.9 fusion.43
  681.3 9.5 convolution_convert_fusion.1
  706.0 13.9 %all-reduce = (f32[2,256]{1,0:T(2,128)}, f32[1024]{0:T(1024)}) all-reduce(f32[2,256]{1,0:T(2,128)S(1)} %pad_maximum_fusion.3, f32[1024]{0:T(1024)S(1)} %copy-done.29), channel_id=1, replica_groups=mesh['fsdp'=8,'tensor'=4] {'fsdp'}, use_global_device_ids=true, to_apply=%region_23.24 | all-reduce | flops 1536 | bytes 12288 | tf_op jit(solution)/shard_map/psum | solution.py:188
  728.1 39.9 %reduce-scatter.26.cloned.1.call-done = bf16[128,768]{1,0:T(8,128)(2,1)} async-done(((bf16[1024,768]{1,0:T(8,128)(2,1)}), bf16[128,768]{1,0:T(8,128)(2,1)}) %reduce-scatter.26.cloned.1.call-update) | async-done | bytes 196624
  770.2 327.2 %all-reduce.10.cloned.1.call-done = (bf16[2308,1024]{1,0:T(8,128)(2,1)}, bf16[2308,1024]{1,0:T(8,128)(2,1)}) async-done(((bf16[2308,1024]{1,0:T(8,128)(2,1)}, bf16[2308,1024]{1,0:T(8,128)(2,1)}), (bf16[2308,1024]{1,0:T(8,128)(2,1)}, bf16[2308,1024]{1,0:T(8,128)(2,1)})) %all-reduce.10.cloned.1.call-update) | async-done | bytes 9453584 | tf_op jit(solution)/shard_map/psum | solution.py:102
  1109.9 13.4 %fusion.15 = f32[2308,1024]{1,0:T(8,128)} fusion(f32[2308,1024]{1,0:T(8,128)} %copy-done, bf16[2308,1024]{1,0:T(8,128)(2,1)} %get-tuple-element.66, f32[2308,1024]{1,0:T(8,128)} %reshape.154, f32[2308]{0:T(1024)S(1)} %broadcast_multiply_fusion.1, f32[2308]{0:T(1024)S(1)} %broadcast_multiply_fusion.2, f32[1024]{0:T(1024)S(1)} %bitcast.99, ...), kind=kLoop, calls=%fused_computation.25 | loop fusion | flops 21270528 | bytes 33128512 | tf_op jit(solution)/shard_map/add | solution.py:160
  1155.7 13.7 %copy.130 = f32[4,577,1024]{2,0,1:T(4,128)} copy(f32[4,577,1024]{2,1,0:T(8,128)} %reshape.153) | data formatting | bytes 18907136
  (225 shorter events, 261.3 us)
Async XLA Ops:
  7.2 54.4 %all-gather.4.cloned.1.call-start = ((), (), s32[]{:S(2)}) async-start(), calls=%async_computation.7 | async-start | bytes 1769472 | tf_op jit(solution)/shard_map/all_gather | solution.py:59
  7.9 303.4 %all-reduce.6.cloned.1.call-start = ((), (), s32[]{:S(2)}) async-start(), calls=%async_computation.8 | async-start | bytes 9469952 | tf_op jit(solution)/shard_map/psum | solution.py:93
  24.8 36.8 %copy-start.16 = (f32[2308]{0:T(1024)}, f32[2308]{0:T(1024)S(1)}, u32[]{:S(2)}) copy-start(f32[2308]{0:T(1024)S(1)} %rsqrt.20) | copy-start | bytes 27700
  24.9 36.7 %copy-start.18 = (f32[2308]{0:T(1024)}, f32[2308]{0:T(1024)S(1)}, u32[]{:S(2)}) copy-start(f32[2308]{0:T(1024)S(1)} %div.27) | copy-start | bytes 27700
  24.9 27.4 %copy-start.22 = (bf16[256,128]{1,0:T(8,128)(2,1)S(1)}, bf16[256,128]{1,0:T(8,128)(2,1)}, u32[]{:S(2)}) copy-start(bf16[256,128]{1,0:T(8,128)(2,1)} %param.18) | copy-start | bytes 196612
  24.9 36.5 %copy-start.36 = (s32[4]{0:T(128)S(1)}, s32[4]{0:T(128)}, u32[]{:S(2)}) copy-start(s32[4]{0:T(128)} %param.13) | copy-start | bytes 52
  61.4 73.2 %copy-start.12 = (bf16[256,1024]{1,0:T(8,128)(2,1)}, bf16[256,1024]{1,0:T(8,128)(2,1)S(1)}, u32[]{:S(2)}) copy-start(bf16[256,1024]{1,0:T(8,128)(2,1)S(1)} %all_gather.24) | copy-start | bytes 1572868
  61.5 59.2 %copy-start.20 = (pred[4,577]{1,0:T(4,128)(4,1)}, pred[4,577]{1,0:T(4,128)(4,1)S(1)}, u32[]{:S(2)}) copy-start(pred[4,577]{1,0:T(4,128)(4,1)S(1)} %iota_compare_fusion) | copy-start | bytes 6928
  85.8 23.6 %copy-start.6 = (bf16[4,577,4,64]{1,3,2,0:T(8,128)(2,1)}, bf16[4,577,4,64]{1,3,2,0:T(8,128)(2,1)S(1)}, u32[]{:S(2)}) copy-start(bf16[4,577,4,64]{1,3,2,0:T(8,128)(2,1)S(1)} %copy.108) | copy-start | bytes 3545092
  98.8 22.0 %copy-start.14 = (bf16[4,577,4,64]{1,0,3,2:T(4,128)(2,1)}, bf16[4,577,4,64]{1,0,3,2:T(4,128)(2,1)S(1)}, u32[]{:S(2)}) copy-start(bf16[4,577,4,64]{1,0,3,2:T(4,128)(2,1)S(1)} %add_convert_fusion.4) | copy-start | bytes 3545092
  134.7 20.4 %copy-start.4 = (bf16[2308,256]{0,1:T(8,128)(2,1)}, bf16[2308,256]{0,1:T(8,128)(2,1)S(1)}, u32[]{:S(2)}) copy-start(bf16[2308,256]{0,1:T(8,128)(2,1)S(1)} %reshape.149) | copy-start | bytes 3545092
  138.2 201.7 %all-gather.6.cloned.1.call-start = ((), (), s32[]{:S(2)}) async-start(), calls=%async_computation.9 | async-start | bytes 2359296 | tf_op jit(solution)/shard_map/all_gather | solution.py:61
  139.0 231.2 %all-gather.8.cloned.1.call-start = ((), (), s32[]{:S(2)}) async-start(), calls=%async_computation.10 | async-start | bytes 2359296 | tf_op jit(solution)/shard_map/all_gather | solution.py:62
  139.6 424.7 %all-reduce.8.cloned.1.call-start = ((), (), s32[]{:S(2)}) async-start(), calls=%async_computation.11 | async-start | bytes 9469952 | tf_op jit(solution)/shard_map/psum | solution.py:118
  391.4 305.1 %reduce-scatter.32.cloned.1.call-start = ((), (), s32[]{:S(2)}) async-start(), calls=%async_computation.18 | async-start | bytes 2359296
  403.2 295.4 %reduce-scatter.20.cloned.1.call-start = ((), (), s32[]{:S(2)}) async-start(), calls=%async_computation.12 | async-start | bytes 2359296 | tf_op jit(solution)/shard_map/reduce_scatter | solution.py:172
  420.7 299.1 %reduce-scatter.30.cloned.1.call-start = ((), (), s32[]{:S(2)}) async-start(), calls=%async_computation.17 | async-start | bytes 294912
  649.7 76.8 %reduce-scatter.28.cloned.1.call-start = ((), (), s32[]{:S(2)}) async-start(), calls=%async_computation.16 | async-start | bytes 589824
  662.1 106.0 %reduce-scatter.26.cloned.1.call-start = ((), (), s32[]{:S(2)}) async-start(), calls=%async_computation.15 | async-start | bytes 1769472
  681.2 416.1 %all-reduce.10.cloned.1.call-start = ((), (), s32[]{:S(2)}) async-start(), calls=%async_computation.19 | async-start | bytes 18939904 | tf_op jit(solution)/shard_map/psum | solution.py:102
  696.4 404.1 %copy-start.17 = (f32[2308]{0:T(1024)S(1)}, f32[2308]{0:T(1024)}, u32[]{:S(2)}) copy-start(f32[2308]{0:T(1024)} %copy-done.16) | copy-start | bytes 27700
  696.4 404.1 %copy-start.19 = (f32[2308]{0:T(1024)S(1)}, f32[2308]{0:T(1024)}, u32[]{:S(2)}) copy-start(f32[2308]{0:T(1024)} %copy-done.18) | copy-start | bytes 27700
  696.4 473.1 %reduce-scatter.22.cloned.1.call-start = ((), (), s32[]{:S(2)}) async-start(), calls=%async_computation.13 | async-start | bytes 294912
  1109.8 69.5 %reduce-scatter.24.cloned.1.call-start = ((), (), s32[]{:S(2)}) async-start(), calls=%async_computation.14 | async-start | bytes 294912
  (31 other events, 295.8 us)
Sparse Core Ops, SparseCore 0:
  9.9 28.2 all-gather.3
  138.4 172.8 all-reduce.5
  313.2 26.7 all-gather.5
  341.7 28.0 all-gather.7
  391.5 172.6 all-reduce.7
  567.3 40.0 reduce-scatter.31
  610.7 41.1 reduce-scatter.19
  655.5 33.6 reduce-scatter.29
  692.3 34.1 reduce-scatter.27
  729.6 38.3 reduce-scatter.25
  771.2 326.0 all-reduce.9
  1109.9 32.6 reduce-scatter.21
  1145.6 33.6 reduce-scatter.23
where the time goes:
time: 1200 us; the launch traced here: 1190 us
  waiting for transfers between devices  691 us (58%)
  matrix products  182 us (15%)
  local copies, waits for them, and re-layouts  142 us (12%)
  other arithmetic  107 us (9%)
  blocking collectives  50.7 us (4%)
  between operations  14.8 us (1%)
    psum x1, waiting for transfers between devices, local(): lax.psum(jnp.dot(activated, full_down, preferred_element_type=jnp.float32...  327 us
    psum x1, waiting for transfers between devices, local(): lax.psum(jnp.dot(attended, full_out, preferred_element_type=jnp.float32)....  150 us
    psum x1, waiting for transfers between devices, local(): lax.psum(jnp.einsum('rf,df->rd', dbefore_b, back_up, preferred_element_ty...  143 us
    unnamed x19, waiting for transfers between devices  55.7 us
    unnamed x106, local copies, waits for them, and re-layouts  53.4 us
    dot_general x1, matrix products, local(): jnp.dot(hidden_two, full_up, preferred_element_type=jnp.float32)  30.2 us
  transfers between devices with their start and end apart: 13, of which 7 were waited for; matrix products, arithmetic and copies ran while one was open for 27% of the time, Pallas kernels for 0%

commit v1 on v0

--- a/solution.py
+++ b/solution.py
@@ -1,14 +1,539 @@
+import functools
+
 import jax
 import jax.numpy as jnp
 from jax import lax
+from jax.experimental import pallas as pl
+from jax.experimental.pallas import tpu as pltpu
 from jax.sharding import PartitionSpec as P
 
 HEAD = 64
-
-
+GROUPS = 8
 epsilon = 1e-06
 half_root = 0.7071067811865476
 density_scale = 0.3989422804014327
+MESH = pl.DeviceIdType.MESH
+bf16 = jnp.bfloat16
+f32 = jnp.float32
+VMEM_LIMIT = 66_500_000
+
+
+def aligned(value, multiple):
+    return pl.multiple_of(value, multiple)
+
+
+class Place:
+    def __init__(self, ratio, length):
+        f = lax.axis_index("fsdp")
+        self.t = lax.axis_index("tensor")
+        self.length = length
+        self.ratio = ratio
+        self.r = lax.rem(f, ratio)
+        g = lax.div(f, ratio)
+        self.g = g
+        self.core = lax.rem(g, 2)
+        self.x = lax.rem(lax.div(g, 2), 2)
+        self.y = lax.div(g, 4)
+        self.gs = self.sib(g)
+        self.gx = g + 2 - 4 * self.x
+        self.gy = g + 4 - 8 * self.y
+        self.gd = self.gx + 4 - 8 * self.y
+
+    def sib(self, g):
+        return g + 1 - 2 * self.core
+
+    def dev(self, g, t):
+        return (g * self.ratio + self.r, t)
+
+    def order(self, i):
+        half = self.length // 2
+        step = 1 - 2 * lax.div(self.t, half)
+        return lax.rem(self.t + i * step + self.length, self.length)
+
+
+def remote(src, dst, send, recv, dev):
+    return pltpu.make_async_remote_copy(
+        src_ref=src, dst_ref=dst, send_sem=send, recv_sem=recv, device_id=dev, device_id_type=MESH
+    )
+
+
+def enter(place, partners):
+    barrier = pltpu.get_barrier_semaphore()
+    count = 0
+    for cond, dev in partners:
+        if cond is None:
+            pl.semaphore_signal(barrier, inc=1, device_id=dev, device_id_type=MESH)
+            count = count + 1
+        else:
+
+            @pl.when(cond)
+            def _(dev=dev):
+                pl.semaphore_signal(barrier, inc=1, device_id=dev, device_id_type=MESH)
+
+            count = count + jnp.where(cond, 1, 0)
+    pl.semaphore_wait(barrier, count)
+
+
+def neighbours(place):
+    g, t = place.g, place.t
+    return [
+        (None, place.dev(place.gs, t)),
+        (None, place.dev(place.gx, t)),
+        (None, place.dev(place.gy, t)),
+        (t < place.length - 1, place.dev(g, t + 1)),
+        (t > 0, place.dev(g, t - 1)),
+    ]
+
+
+def piece(kind, ref, g, t, n, half=None):
+    size = n if half is None else n // 2
+    off = 0 if half in (None, 0) else n // 2
+    if kind == "q":
+        return ref.at[:, t, pl.ds(aligned(g * n + off, size), size), :]
+    if kind == "u":
+        return ref.at[t, pl.ds(aligned(g * n + off, size), size), :]
+    if kind in ("o", "d"):
+        return ref.at[g, pl.ds(aligned(t * n + off, size), size), :]
+    return ref.at[g, t, pl.ds(off, size), :]
+
+
+class Gather:
+    def __init__(self, place, index, kind, shard, full, n, sems):
+        self.p, self.a, self.kind, self.shard, self.full, self.n = place, index, kind, shard, full, n
+        self.s_z, self.s_xy, self.s_sib, self.r_z, self.r_xy, self.r_sib, self.loc = sems
+
+    def view(self, g, o, half=None):
+        return piece(self.kind, self.full, g, o, self.n, half)
+
+    def put(self, src, g, o, half, send, recv, dev):
+        return remote(src, self.view(g, o, half), send, recv, dev)
+
+    def c_up(self, src, o):
+        p = self.p
+        return self.put(src, p.g, o, None, self.s_z.at[self.a, 0, o], self.r_z.at[self.a, o], p.dev(p.g, p.t + 1))
+
+    def c_down(self, src, o):
+        p = self.p
+        return self.put(src, p.g, o, None, self.s_z.at[self.a, 1, o], self.r_z.at[self.a, o], p.dev(p.g, p.t - 1))
+
+    def c_xy(self, src, which, o):
+        p = self.p
+        g = (p.g, p.g, p.gx, p.gy)[which]
+        half = (None, None, 0, 1)[which]
+        to = (p.gx, p.gy, p.gy, p.gx)[which]
+        return self.put(src, g, o, half, self.s_xy.at[self.a, which, o], self.r_xy.at[self.a, which, o], p.dev(to, p.t))
+
+    def c_sib(self, src, which, o):
+        p = self.p
+        g = (p.g, p.gx, p.gy, p.gd, p.gd)[which]
+        half = (None, None, None, 0, 1)[which]
+        return self.put(src, g, o, half, self.s_sib.at[self.a, which, o], self.r_sib.at[self.a, which, o], p.dev(p.gs, p.t))
+
+    def own(self):
+        p = self.p
+        src, t = self.shard, p.t
+        pltpu.make_async_copy(src, self.view(p.g, t), self.loc.at[self.a]).start()
+
+        @pl.when(t < p.length - 1)
+        def _():
+            self.c_up(src, t).start()
+
+        @pl.when(t > 0)
+        def _():
+            self.c_down(src, t).start()
+
+        self.c_xy(src, 0, t).start()
+        self.c_xy(src, 1, t).start()
+        self.c_sib(src, 0, t).start()
+
+    def spread(self, o):
+        src = self.view(self.p.g, o)
+        self.c_xy(src, 0, o).start()
+        self.c_xy(src, 1, o).start()
+        self.c_sib(src, 0, o).start()
+
+    def z(self, d):
+        p = self.p
+        t, last = p.t, p.length - 1
+
+        @pl.when(t - d >= 0)
+        def _():
+            o = t - d
+            src = self.view(p.g, o)
+            self.c_up(src, o).wait_recv()
+
+            @pl.when(t < last)
+            def _():
+                self.c_up(src, o).start()
+
+            self.spread(o)
+
+        @pl.when(t + d <= last)
+        def _():
+            o = t + d
+            src = self.view(p.g, o)
+            self.c_down(src, o).wait_recv()
+
+            @pl.when(t > 0)
+            def _():
+                self.c_down(src, o).start()
+
+            self.spread(o)
+
+    def side(self, which, i):
+        p = self.p
+        o = p.order(i)
+        g = (p.gx, p.gy)[which]
+        full = self.view(g, o)
+        self.wait_xy(which, g, o, None)
+        self.c_xy(self.view(g, o, which), 2 + which, o).start()
+        self.c_sib(full, 1 + which, o).start()
+
+    def wait_xy(self, which, g, o, half):
+        v = self.view(g, o, half)
+        p = self.p
+        remote(v, v, self.s_xy.at[self.a, which, o], self.r_xy.at[self.a, which, o], p.dev(p.gx, p.t)).wait_recv()
+
+    def diag(self, which, i):
+        p = self.p
+        o = p.order(i)
+        self.wait_xy(2 + which, p.gd, o, which)
+        self.c_sib(self.view(p.gd, o, which), 3 + which, o).start()
+
+    def finish(self):
+        p = self.p
+
+        @pl.loop(0, p.length)
+        def _(o):
+            for which in range(5):
+                g = p.sib((p.g, p.gx, p.gy, p.gd, p.gd)[which])
+                half = (None, None, None, 0, 1)[which]
+                v = self.view(g, o, half)
+                remote(v, v, self.s_sib.at[self.a, which, o], self.r_sib.at[self.a, which, o], p.dev(p.gs, p.t)).wait_recv()
+
+        pltpu.make_async_copy(self.shard, self.view(p.g, p.t), self.loc.at[self.a]).wait()
+
+    def drain(self):
+        p = self.p
+
+        @pl.loop(0, p.length)
+        def _(o):
+            src = self.view(p.g, o)
+
+            @pl.when(jnp.logical_and(o <= p.t, p.t < p.length - 1))
+            def _():
+                self.c_up(src, o).wait_send()
+
+            @pl.when(jnp.logical_and(o >= p.t, p.t > 0))
+            def _():
+                self.c_down(src, o).wait_send()
+
+            self.c_xy(src, 0, o).wait_send()
+            self.c_xy(src, 1, o).wait_send()
+            self.c_xy(self.view(p.gx, o, 0), 2, o).wait_send()
+            self.c_xy(self.view(p.gy, o, 1), 3, o).wait_send()
+            for which in range(5):
+                g = (p.g, p.gx, p.gy, p.gd, p.gd)[which]
+                half = (None, None, None, 0, 1)[which]
+                self.c_sib(self.view(g, o, half), which, o).wait_send()
+
+    def middle(self):
+        for d in range(1, self.p.length):
+            yield self.z(d)
+        for i in range(self.p.length):
+            yield self.side(0, i)
+            yield self.side(1, i)
+        for i in range(self.p.length):
+            yield self.diag(0, i)
+            yield self.diag(1, i)
+
+
+def gather_sems(arrays, length):
+    dma = pltpu.SemaphoreType.DMA
+    return [
+        dma((arrays, 2, length)),
+        dma((arrays, 4, length)),
+        dma((arrays, 5, length)),
+        dma((arrays, length)),
+        dma((arrays, 4, length)),
+        dma((arrays, 5, length)),
+        dma((arrays,)),
+    ]
+
+
+def step(gen, count=1):
+    for _ in range(count):
+        next(gen, None)
+
+
+def chain(*gens):
+    for g in gens:
+        yield from g
+
+
+def statistics(tokens):
+    average = jnp.mean(tokens, axis=-1, keepdims=True)
+    centred = tokens - average
+    inverse = lax.rsqrt(jnp.mean(centred * centred, axis=-1, keepdims=True) + epsilon)
+    return centred * inverse, inverse
+
+
+def nt(a, b):
+    return lax.dot_general(a, b, (((1,), (1,)), ((), ())), preferred_element_type=f32)
+
+
+def tn(a, b):
+    return lax.dot_general(a, b, (((0,), (0,)), ((), ())), preferred_element_type=f32)
+
+
+def nn(a, b):
+    return jnp.dot(a, b, preferred_element_type=f32)
+
+
+def wide(ref, lead, rows=slice(None)):
+    return jnp.concatenate([ref[i, rows, :] for i in lead], axis=1)
+
+
+def store_out(copies, src, dst, sem):
+    c = pltpu.make_async_copy(src, dst, sem)
+    c.start()
+    copies.append(c)
+
+
+def forward_kernel(ratio, length, x, mask, s_s, q_s, o_s, u_s, d_s,
+                   vec_o, wq_o, wo_o, wu_o, wd_o, hid1_o, qkv_o, att_o, lse_o, mid_o, hid2_o, act_o, g_o, out_o,
+                   ws, wq, wo, wu, wd, smf, vec, hid1, qkv, att, lse, mid, hid2, act, gg, pre, outb,
+                   s_z, s_xy, s_sib, r_z, r_xy, r_sib, loc, outs):
+    place = Place(ratio, length)
+    rows, width = hid1.shape
+    keys = qkv.shape[1]
+    hidden = act.shape[1]
+    nb = rows // 16
+    sems = (s_z, s_xy, s_sib, r_z, r_xy, r_sib, loc)
+    small = Gather(place, 0, "s", s_s, ws, s_s.shape[0], sems)
+    gq = Gather(place, 1, "q", q_s, wq, q_s.shape[1], sems)
+    go = Gather(place, 2, "o", o_s, wo, o_s.shape[0], sems)
+    gu = Gather(place, 3, "u", u_s, wu, u_s.shape[0], sems)
+    gd = Gather(place, 4, "d", d_s, wd, d_s.shape[0], sems)
+    everything = (small, gq, go, gu, gd)
+    enter(place, neighbours(place))
+    small.own()
+    gq.own()
+    go.own()
+    for _ in small.middle():
+        pass
+    gu.own()
+    first = gq.middle()
+    step(first, 3)
+    small.finish()
+    copies = []
+
+    for g in range(GROUPS):
+        for t in range(length):
+            smf[g, t] = ws[g, t].astype(f32)
+    per = width // GROUPS
+    for row in range(6):
+        vec[row : row + 1, 0:width] = jnp.concatenate([smf[g, 0, row : row + 1, :] for g in range(GROUPS)], axis=1)
+    local = width // length
+    for c in range(2):
+        parts = []
+        for t in range(length):
+            for j in range(local // 128):
+                r = 6 + c * (local // 128) + j
+                parts.append(smf[0, t, r : r + 1, :])
+        vec[6 + c : 7 + c, 0:width] = jnp.concatenate(parts, axis=1)
+    base = 6 + 2 * (local // 128)
+    nh = hidden // length // 128
+    for t in range(length):
+        vec[8 : 9, t * (hidden // length) : (t + 1) * (hidden // length)] = jnp.concatenate(
+            [smf[0, t, base + j : base + j + 1, :] for j in range(nh)], axis=1
+        )
+    store_out(copies, vec, vec_o, outs.at[13])
+
+    gain, shift = vec[0:1, 0:width], vec[2:3, 0:width]
+
+    @pl.loop(0, nb)
+    def _(i):
+        r = pl.ds(aligned(i * 16, 16), 16)
+        n, _inv = statistics(x[r, :].astype(f32))
+        hid1[r, :] = (n * gain + shift).astype(bf16)
+
+    store_out(copies, hid1, hid1_o, outs.at[0])
+    qkv[:, rows:keys, :] = jnp.zeros((3, keys - rows, width), bf16)
+    for _ in first:
+        pass
+    second = chain(go.middle(), gu.middle(), gd.middle())
+    step(second, 3)
+    gq.finish()
+    store_out(copies, wq, wq_o, outs.at[1])
+    step(second, 8)
+    gd.own()
+
+    scale = HEAD ** (-0.5)
+    for c in range(3):
+        r = nn(hid1[...], wide(wq.at[c], range(length)))
+        if c == 0:
+            r = (r + vec[6:7, 0:width]).astype(bf16) * jnp.asarray(scale, bf16)
+        elif c == 2:
+            r = (r + vec[7:8, 0:width]).astype(bf16)
+        else:
+            r = r.astype(bf16)
+        qkv[c, 0:rows, :] = r
+        step(second, 3)
+    store_out(copies, qkv, qkv_o, outs.at[2])
+
+    pairs = width // 128
+    low = lax.broadcasted_iota(jnp.int32, (128, 128), 1) < HEAD
+
+    def attend(p):
+        cols = pl.ds(aligned(p * 128, 128), 128)
+        k2 = qkv[1, :, cols]
+        v2 = qkv[2, :, cols]
+        for r0 in range(0, keys, 128):
+            n = min(128, rows - r0)
+            q2 = qkv[0, r0 : r0 + 128, cols]
+            done = []
+            for h in range(2):
+                mine = low if h == 0 else jnp.logical_not(low)
+                s = nt(jnp.where(mine, q2, jnp.zeros_like(q2)), k2) + mask[...]
+                m = jnp.max(s, axis=-1, keepdims=True)
+                e = jnp.exp(s - m)
+                total = jnp.sum(e, axis=-1, keepdims=True)
+                done.append(nn(e.astype(bf16), v2) * (1.0 / total))
+                flat = jnp.transpose(jnp.broadcast_to(m + jnp.log(total), (128, 128)))
+                lse[p, h : h + 1, r0 : r0 + 128] = flat[0:1, :]
+            a2 = jnp.where(low, done[0], done[1]).astype(bf16)
+            att[r0 : r0 + n, cols] = a2[0:n, :]
+
+    for part in range(4):
+
+        @pl.loop(0, pairs // 4)
+        def _(j):
+            attend(part * (pairs // 4) + j)
+
+        step(second, 6)
+    store_out(copies, att, att_o, outs.at[3])
+    store_out(copies, lse, lse_o, outs.at[4])
+    go.finish()
+    store_out(copies, wo, wo_o, outs.at[5])
+    step(second, 2)
+
+    mid[...] = nn(att[...], wide(wo, range(GROUPS))) + vec[4:5, 0:width]
+    step(second, 2)
+    gain2, shift2 = vec[1:2, 0:width], vec[3:4, 0:width]
+
+    @pl.loop(0, nb)
+    def _(i):
+        r = pl.ds(aligned(i * 16, 16), 16)
+        m = x[r, :].astype(f32) + mid[r, :]
+        mid[r, :] = m
+        n, _inv = statistics(m)
+        hid2[r, :] = (n * gain2 + shift2).astype(bf16)
+
+    store_out(copies, mid, mid_o, outs.at[6])
+    store_out(copies, hid2, hid2_o, outs.at[7])
+    left = length * 4 + length - 1
+    for _ in range(200):
+        step(second)
+    gu.finish()
+    store_out(copies, wu, wu_o, outs.at[8])
+
+    part = pre.shape[1]
+    for t in range(hidden // part):
+        cols = slice(t * part, (t + 1) * part)
+        each = wu.shape[2]
+        blk, off = (t * part) // each, (t * part) % each
+        pre[...] = nn(hid2[...], wu[blk, :, off : off + part])
+
+        @pl.loop(0, nb)
+        def _(i):
+            r = pl.ds(aligned(i * 16, 16), 16)
+            z = pre[r, :] + vec[8:9, cols]
+            cdf = 0.5 * (1.0 + lax.erf(z * half_root))
+            act[r, cols] = (z * cdf).astype(bf16)
+            gg[r, cols] = (cdf + z * (jnp.exp(-0.5 * z * z) * density_scale)).astype(bf16)
+
+    store_out(copies, act, act_o, outs.at[9])
+    store_out(copies, gg, g_o, outs.at[10])
+    gd.finish()
+    store_out(copies, wd, wd_o, outs.at[11])
+
+    for j in range(GROUPS // 2):
+        cols = slice(2 * j * per, 2 * (j + 1) * per)
+        r = nn(act[...], wide(wd, (2 * j, 2 * j + 1)))
+        outb[:, cols] = (mid[:, cols] + (r + vec[5:6, cols])).astype(bf16)
+    store_out(copies, outb, out_o, outs.at[12])
+    for a in everything:
+        a.drain()
+    for c in copies:
+        c.wait()
+
+
+def any_spec():
+    return pl.BlockSpec(memory_space=pl.ANY)
+
+
+def vmem_spec():
+    return pl.BlockSpec(memory_space=pltpu.VMEM)
+
+
+def forward(ratio, length, x, mask, small, q_s, o_s, u_s, d_s):
+    rows, width = x.shape
+    keys = mask.shape[1]
+    hidden = u_s.shape[1] * length
+    sds = jax.ShapeDtypeStruct
+    n_q, n_o, n_u, n_d = q_s.shape[1], o_s.shape[0], u_s.shape[0], d_s.shape[0]
+    wq = ((3, length, GROUPS * n_q, q_s.shape[2]), bf16)
+    wo = ((GROUPS, length * n_o, o_s.shape[1]), bf16)
+    wu = ((length, GROUPS * n_u, u_s.shape[1]), bf16)
+    wd = ((GROUPS, length * n_d, d_s.shape[1]), bf16)
+    pairs = width // 128
+    vec = ((16, hidden), f32)
+    hid = ((rows, width), bf16)
+    qkv = ((3, keys, width), bf16)
+    lse = ((pairs, 8, keys), f32)
+    mid = ((rows, width), f32)
+    act = ((rows, hidden), bf16)
+    outs = [vec, wq, wo, wu, wd, hid, qkv, hid, lse, mid, hid, act, act, hid]
+    scratch = [((GROUPS, length) + small.shape, bf16), wq, wo, wu, wd, ((GROUPS, length) + small.shape, f32), vec,
+               hid, qkv, hid, lse, mid, hid, act, act, ((rows, 512), f32), hid]
+    return pl.pallas_call(
+        functools.partial(forward_kernel, ratio, length),
+        out_shape=[sds(*o) for o in outs],
+        in_specs=[vmem_spec(), vmem_spec()] + [any_spec()] * 5,
+        out_specs=[any_spec()] * len(outs),
+        scratch_shapes=[pltpu.VMEM(*s) for s in scratch] + gather_sems(5, length) + [pltpu.SemaphoreType.DMA((14,))],
+        compiler_params=pltpu.CompilerParams(collective_id=0, has_side_effects=True, vmem_limit_bytes=VMEM_LIMIT),
+        name="forward",
+    )(x, mask, small, q_s, o_s, u_s, d_s)
+
+
+def prepare(length, inputs, lengths, norm_gains, norm_shifts, w_qkv, bias_qv, w_out, out_bias, w_up, b_up, w_down, cotangent, fsdp):
+    ratio = fsdp // GROUPS
+    if ratio > 1:
+        groups = [[g * ratio + r for r in range(ratio)] for g in range(GROUPS)]
+
+        def join(a, axis):
+            return lax.all_gather(a, "fsdp", axis=axis, tiled=True, axis_index_groups=groups)
+
+        norm_gains, norm_shifts, out_bias = join(norm_gains, 1), join(norm_shifts, 1), join(out_bias, 1)
+        w_qkv, w_out, w_up, w_down = join(w_qkv, 1), join(w_out, 1), join(w_up, 0), join(w_down, 1)
+    t = lax.axis_index("tensor")
+    batch, seq, width = inputs.shape
+    rows = -(-seq // 16) * 16
+    keys = -(-seq // 128) * 128
+
+    def mine(a):
+        a = lax.dynamic_index_in_dim(a, t, 0, keepdims=False)
+        return jnp.pad(a, ((0, rows - seq), (0, 0)))
+
+    count = lax.dynamic_index_in_dim(lengths, t, 0, keepdims=False)
+    mask = jnp.where(jnp.arange(keys) < count, 0.0, -jnp.inf).astype(f32)
+    small = jnp.concatenate(
+        [norm_gains, norm_shifts, out_bias, bias_qv.reshape(-1, 128), b_up.reshape(-1, 128)], axis=0
+    )
+    small = jnp.pad(small, ((0, 32 - small.shape[0]), (0, 0)))
+    return ratio, mine(inputs), mine(cotangent), mask, small, w_qkv, w_out, w_up, w_down
 
 
 def normalize(tokens):
@@ -103,7 +628,11 @@
         jnp.dot(activated, full_down, preferred_element_type=jnp.float32).astype(jnp.bfloat16),
         "tensor",
     ).astype(jnp.float32)
-    result = (middle + (mlp_total + bias_rows[1])).astype(jnp.bfloat16)
+    ratio, x_own, _ct, mask, small, q_s, o_s, u_s, d_s = prepare(
+        w_qkv.shape[2] and lax.axis_size("tensor"), inputs, lengths, norm_gains, norm_shifts, w_qkv, bias_qv, w_out, out_bias,
+        w_up, b_up, w_down, cotangent, lax.axis_size("fsdp"))
+    own = forward(ratio, lax.axis_size("tensor"), x_own, mask[None, :], small, q_s, o_s, u_s, d_s)[-1]
+    result = lax.all_gather(own[:seq_len], "tensor", axis=0)
     back_qkv, back_out, back_up, back_down = (full_qkv, full_out, full_up, full_down)
     grad_rows = cotangent.reshape(tokens, width)
     grad_f = grad_rows.astype(jnp.float32)

time: 1200 us -> 1190 us (level)
  Pallas kernels: 0 us -> 224 us
  waiting for transfers between devices: 691 us -> 470 us
    pallas_call x0 -> x1, Pallas kernels: none -> 224 us  [forward(): pl.pallas_call(functools.partial(forward_kernel, ratio, length), out_shap...]
    psum x1, waiting for transfers between devices: 327 us -> 173 us  [local(): lax.psum(jnp.einsum('cre,cde->rd', stacked, back_qkv, preferred_element_t...]
    psum x1, waiting for transfers between devices: 143 us -> 0.02 us  [local(): lax.psum(jnp.einsum('rf,df->rd', dbefore_b, back_up, preferred_element_ty...]
    unnamed x19 -> x20, waiting for transfers between devices: 55.7 us -> 117 us
    dot_general x1, matrix products: 30.2 us -> 10.1 us  [local(): jnp.dot(hidden_two, full_up, preferred_element_type=jnp.float32)]
    all_gather x1, waiting for transfers between devices: 0.01 us -> 19.7 us  [local(): lax.all_gather(w_down, 'fsdp', axis=1, tiled=True)]
    dot_general x1, matrix products: 9.07 us -> 27.9 us  [local(): jnp.einsum('rf,rd->fd', activated, grad_rows, preferred_element_type=jnp....]
    unnamed x106 -> x100, local copies, waits for them, and re-layouts: 53.4 us -> 58.6 us
  transfers between devices with their start and end apart: 13 -> 14, of which waited for: 7 -> 8; matrix products, arithmetic and copies ran while one was open for 27% -> 27% of each run, Pallas kernels for 0% -> 19%
where the time goes in v1:
time: 1190 us; the launch traced here: 1180 us
  waiting for transfers between devices  470 us (39%)
  Pallas kernels  224 us (19%)
  matrix products  171 us (14%)
  local copies, waits for them, and re-layouts  148 us (12%)
  other arithmetic  101 us (8%)
  blocking collectives  49.6 us (4%)
  between operations  15.1 us (1%)
    pallas_call x1, Pallas kernels, forward(): pl.pallas_call(functools.partial(forward_kernel, ratio, length), out_shap...  224 us
    psum x1, waiting for transfers between devices, local(): lax.psum(jnp.einsum('cre,cde->rd', stacked, back_qkv, preferred_element_t...  173 us
    psum x1, waiting for transfers between devices, local(): lax.psum(jnp.dot(attended, full_out, preferred_element_type=jnp.float32)....  151 us
    unnamed x20, waiting for transfers between devices  117 us
    unnamed x100, local copies, waits for them, and re-layouts  58.6 us
    dot_general x1, matrix products, local(): jnp.einsum('rf,rd->fd', activated, grad_rows, preferred_element_type=jnp....  27.9 us
  transfers between devices with their start and end apart: 14, of which 8 were waited for; matrix products, arithmetic and copies ran while one was open for 27% of the time, Pallas kernels for 19%

profile of v1, /device:TPU:0, one launch (start us, length us, event | category | flops | bytes accessed | tf_op | source)
XLA Modules:
  0.0 1180.1 jit_solution(6892874963566259434)
XLA Ops:
  34.9 10.2 all_gather.29
  53.9 9.2 all_gather.32
  97.7 10.7 fusion.1
  108.4 11.3 exponential_reduce_fusion
  120.4 11.0 convolution_convert_fusion.5
  160.3 150.9 %all-reduce.7.cloned.1.call-done = bf16[2308,1024]{1,0:T(8,128)(2,1)} async-done(((bf16[2308,1024]{1,0:T(8,128)(2,1)}), bf16[2308,1024]{1,0:T(8,128)(2,1)}) %all-reduce.7.cloned.1.call-update) | async-done | bytes 4726800 | tf_op jit(solution)/shard_map/psum | solution.py:618
  311.2 9.8 fusion.101
  339.9 10.1 fusion.106
  350.0 19.7 %all-gather.9.cloned.1.call-done = bf16[1024,1024]{1,0:T(8,128)(2,1)} async-done(((bf16[1024,128]{1,0:T(8,128)(2,1)}), bf16[1024,1024]{1,0:T(8,128)(2,1)}) %all-gather.9.cloned.1.call-update) | async-done | bytes 2097168 | tf_op jit(solution)/shard_map/all_gather | solution.py:587
  369.7 12.1 %fusion.105 = (f32[1024]{0:T(1024)}, bf16[2308,1024]{1,0:T(8,128)(2,1)S(1)}) fusion(f32[2308,1024]{1,0:T(8,128)} %fusion.106, f32[1024]{0:T(1024)S(1)} %convert_element_type.152, bf16[2308,1024]{1,0:T(8,128)(2,1)} %reshape.164, bf16[1024,1024]{1,0:T(8,128)(2,1)} %all-gather.9.cloned.1.call-done), kind=kOutput, calls=%fused_computation.160 | convolution fusion | flops 4868586496 | bytes 21012480 | tf_op jit(solution)/shard_map/rd,fd->rf/dot_general | solution.py:640
  399.8 224.5 %forward.1 = (f32[16,4096]{1,0:T(8,128)}, bf16[3,4,1024,256]{3,2,1,0:T(8,128)(2,1)}, bf16[8,1024,128]{2,1,0:T(8,128)(2,1)}, bf16[4,1024,1024]{2,1,0:T(8,128)(2,1...) custom-call(bf16[592,1024]{1,0:T(8,128)(2,1)} %pad.8.x, ...), custom_call_target="tpu_custom_call" | custom-call | tf_op jit(solution)/shard_map/forward/pallas_call | solution.py:500
  626.8 27.9 %fusion.45 = bf16[1024,1024]{1,0:T(8,128)(2,1)S(1)} fusion(bf16[2308,1024]{1,0:T(8,128)(2,1)} %reshape.164, f32[2308,1024]{1,0:T(8,128)} %fusion.106, f32[1024]{0:T(1024)S(1)} %convert_element_type.152), kind=kOutput, calls=%fused_computation.81 | convolution fusion | flops 4997259264 | bytes 16281600 | tf_op jit(solution)/shard_map/rf,rd->fd/dot_general | solution.py:639
  661.7 9.9 fusion.42
  700.9 17.1 %multiply_convert_fusion = bf16[4,4,577,577]{2,3,1,0:T(8,128)(2,1)} fusion(f32[4,4,577,577]{2,3,1,0:T(8,128)} %get-tuple-element.78, f32[4,4,577]{2,1,0:T(4,128)S(1)} %multiply_reduce_fusion.2, f32[4,4,577]{2,1,0:T(4,128)S(1)} %bitcast.101, pred[4,577]{1,0:T(4,128)(4,1)S(1)} %copy-done.23, bf16[4,577,4,64]{1,0,3,2:T(4,128)(2,1)} %reshape.166, ...), kind=kOutput, calls=%fused_computation | convolution fusion | flops 719126592 | bytes 34400740 | tf_op jit(solution)/shard_map/bqhe,bkhe->bhqk/dot_general | solution.py:664
  744.9 12.3 %bitcast_convert_fusion.1 = (bf16[4,577,4,64]{1,3,2,0:T(8,128)(2,1)}, f32[4,4,64,577]{3,2,1,0:T(8,128)}) fusion(f32[4,4,577,577]{2,3,1,0:T(8,128)} %get-tuple-element.78, f32[4,4,577]{2,1,0:T(4,128)S(1)} %bitcast.102, pred[4,577]{1,0:T(4,128)(4,1)S(1)} %copy-done.23, bf16[4,577,4,64]{1,0,3,2:T(4,128)(2,1)S(1)} %copy-done.13), kind=kOutput, calls=%fused_computation.67 | convolution fusion | flops 703736896 | bytes 26073476 | tf_op jit(solution)/shard_map/bhqk,bqhe->bkhe/dot_general | solution.py:677
  773.0 11.5 fusion.48
  815.6 12.7 %all-reduce.2 = (f32[2,256]{1,0:T(2,128)}, f32[1024]{0:T(1024)}) all-reduce(f32[2,256]{1,0:T(2,128)S(1)} %pad_maximum_fusion.3, f32[1024]{0:T(1024)S(1)} %copy-done.30), channel_id=1, replica_groups=mesh['fsdp'=8,'tensor'=4] {'fsdp'}, use_global_device_ids=true, to_apply=%region_22.23 | all-reduce | flops 1536 | bytes 12288 | tf_op jit(solution)/shard_map/psum | solution.py:717
  828.3 15.8 %reduce-scatter.30.cloned.1.call-done = bf16[128,2]{1,0:T(8,128)(2,1)} async-done(((bf16[1024,2]{1,0:T(8,128)(2,1)}), bf16[128,2]{1,0:T(8,128)(2,1)}) %reduce-scatter.30.cloned.1.call-update) | async-done | bytes 528
  845.5 35.6 %reduce-scatter.28.cloned.1.call-done = bf16[128,256]{1,0:T(8,128)(2,1)} async-done(((bf16[1024,256]{1,0:T(8,128)(2,1)}), bf16[128,256]{1,0:T(8,128)(2,1)}) %reduce-scatter.28.cloned.1.call-update) | async-done | bytes 65552
  882.8 40.1 %reduce-scatter.26.cloned.1.call-done = bf16[128,768]{1,0:T(8,128)(2,1)} async-done(((bf16[1024,768]{1,0:T(8,128)(2,1)}), bf16[128,768]{1,0:T(8,128)(2,1)}) %reduce-scatter.26.cloned.1.call-update) | async-done | bytes 196624
  925.0 173.4 %all-reduce.11.cloned.1.call-done = bf16[2308,1024]{1,0:T(8,128)(2,1)} async-done(((bf16[2308,1024]{1,0:T(8,128)(2,1)}), bf16[2308,1024]{1,0:T(8,128)(2,1)}) %all-reduce.11.cloned.1.call-update) | async-done | bytes 4726800 | tf_op jit(solution)/shard_map/psum | solution.py:683
  1112.0 13.0 %fusion.15 = f32[2308,1024]{1,0:T(8,128)} fusion(f32[2308,1024]{1,0:T(8,128)} %copy-done.1, bf16[2308,1024]{1,0:T(8,128)(2,1)} %all-reduce.11.cloned.1.call-done, f32[2308,1024]{1,0:T(8,128)} %reshape.168, f32[2308]{0:T(1024)S(1)} %broadcast_multiply_fusion.1, f32[2308]{0:T(1024)S(1)} %broadcast_multiply_fusion.2, f32[1024]{0:T(1024)S(1)} %bitcast.106, ...), kind=kLoop, calls=%fused_computation.25 | loop fusion | flops 21270528 | bytes 33128512 | tf_op jit(solution)/shard_map/add | solution.py:689
  1133.5 13.6 %copy.133 = f32[4,577,1024]{2,0,1:T(4,128)} copy(f32[4,577,1024]{2,1,0:T(8,128)} %reshape.167) | data formatting | bytes 18907136
  1148.5 23.3 %reduce-scatter.22.cloned.1.call-done = bf16[128,2]{1,0:T(8,128)(2,1)} async-done(((bf16[1024,2]{1,0:T(8,128)(2,1)}), bf16[128,2]{1,0:T(8,128)(2,1)}) %reduce-scatter.22.cloned.1.call-update) | async-done | bytes 528
  (227 shorter events, 279.2 us)
Async XLA Ops:
  7.2 56.1 %all-gather.7.cloned.1.call-start = ((), (), s32[]{:S(2)}) async-start(), calls=%async_computation.7 | async-start | bytes 1769472 | tf_op jit(solution)/shard_map/all_gather | solution.py:584
  7.9 303.3 %all-reduce.7.cloned.1.call-start = ((), (), s32[]{:S(2)}) async-start(), calls=%async_computation.8 | async-start | bytes 9469952 | tf_op jit(solution)/shard_map/psum | solution.py:618
  24.0 21.1 %copy-start.32 = (bf16[2,128]{1,0:T(2,128)(2,1)S(1)}, bf16[2,128]{1,0:T(2,128)(2,1)}, u32[]{:S(2)}) copy-start(bf16[2,128]{1,0:T(2,128)(2,1)} %param.15) | copy-start | bytes 1540
  24.0 29.9 %copy-start.17 = (bf16[256,128]{1,0:T(8,128)(2,1)S(1)}, bf16[256,128]{1,0:T(8,128)(2,1)}, u32[]{:S(2)}) copy-start(bf16[256,128]{1,0:T(8,128)(2,1)} %o_s.1) | copy-start | bytes 196612
  24.0 39.1 %copy-start.35 = (s32[4]{0:T(128)S(1)}, s32[4]{0:T(128)}, u32[]{:S(2)}) copy-start(s32[4]{0:T(128)} %param.13) | copy-start | bytes 52
  34.6 36.6 %copy-start.18 = (f32[2308]{0:T(1024)}, f32[2308]{0:T(1024)S(1)}, u32[]{:S(2)}) copy-start(f32[2308]{0:T(1024)S(1)} %rsqrt.20) | copy-start | bytes 27700
  34.7 36.5 %copy-start.20 = (f32[2308]{0:T(1024)}, f32[2308]{0:T(1024)S(1)}, u32[]{:S(2)}) copy-start(f32[2308]{0:T(1024)S(1)} %div.27) | copy-start | bytes 27700
  63.1 71.4 %copy-start.14 = (bf16[256,1024]{1,0:T(8,128)(2,1)}, bf16[256,1024]{1,0:T(8,128)(2,1)S(1)}, u32[]{:S(2)}) copy-start(bf16[256,1024]{1,0:T(8,128)(2,1)S(1)} %all_gather.32) | copy-start | bytes 1572868
  63.2 57.2 %copy-start.22 = (pred[4,577]{1,0:T(4,128)(4,1)}, pred[4,577]{1,0:T(4,128)(4,1)S(1)}, u32[]{:S(2)}) copy-start(pred[4,577]{1,0:T(4,128)(4,1)S(1)} %iota_compare_fusion) | copy-start | bytes 6928
  138.2 201.7 %all-gather.11.cloned.1.call-start = ((), (), s32[]{:S(2)}) async-start(), calls=%async_computation.10 | async-start | bytes 2359296 | tf_op jit(solution)/shard_map/all_gather | solution.py:586
  138.9 230.8 %all-gather.9.cloned.1.call-start = ((), (), s32[]{:S(2)}) async-start(), calls=%async_computation.9 | async-start | bytes 2359296 | tf_op jit(solution)/shard_map/all_gather | solution.py:587
  139.5 532.2 %all-reduce.9.cloned.1.call-start = ((), (), s32[]{:S(2)}) async-start(), calls=%async_computation.11 | async-start | bytes 9469952 | tf_op jit(solution)/shard_map/psum | solution.py:647
  350.0 34.0 %copy-start.36 = (bf16[1024,1024]{1,0:T(8,128)(2,1)S(1)}, bf16[1024,1024]{1,0:T(8,128)(2,1)}, u32[]{:S(2)}) copy-start(bf16[1024,1024]{1,0:T(8,128)(2,1)} %all-gather.11.cloned.1.call-done) | copy-start | bytes 6291460
  390.8 407.2 %all-gather.13.cloned.1.call-start = ((), (), s32[]{:S(2)}) async-start(), calls=%async_computation.14 | async-start | bytes 5980160 | tf_op jit(solution)/shard_map/all_gather | solution.py:635
  626.7 179.6 %reduce-scatter.32.cloned.1.call-start = ((), (), s32[]{:S(2)}) async-start(), calls=%async_computation.20 | async-start | bytes 2359296
  657.3 151.0 %reduce-scatter.20.cloned.1.call-start = ((), (), s32[]{:S(2)}) async-start(), calls=%async_computation.13 | async-start | bytes 2359296 | tf_op jit(solution)/shard_map/reduce_scatter | solution.py:701
  671.6 172.4 %reduce-scatter.30.cloned.1.call-start = ((), (), s32[]{:S(2)}) async-start(), calls=%async_computation.19 | async-start | bytes 294912
  757.2 124.0 %reduce-scatter.28.cloned.1.call-start = ((), (), s32[]{:S(2)}) async-start(), calls=%async_computation.18 | async-start | bytes 589824
  769.5 153.4 %reduce-scatter.26.cloned.1.call-start = ((), (), s32[]{:S(2)}) async-start(), calls=%async_computation.17 | async-start | bytes 1769472
  789.1 309.3 %all-reduce.11.cloned.1.call-start = ((), (), s32[]{:S(2)}) async-start(), calls=%async_computation.12 | async-start | bytes 9469952 | tf_op jit(solution)/shard_map/psum | solution.py:683
  798.0 349.1 %reduce-scatter.24.cloned.1.call-start = ((), (), s32[]{:S(2)}) async-start(), calls=%async_computation.16 | async-start | bytes 294912
  807.5 295.2 %copy-start.19 = (f32[2308]{0:T(1024)S(1)}, f32[2308]{0:T(1024)}, u32[]{:S(2)}) copy-start(f32[2308]{0:T(1024)} %copy-done.18) | copy-start | bytes 27700
  807.5 295.2 %copy-start.21 = (f32[2308]{0:T(1024)S(1)}, f32[2308]{0:T(1024)}, u32[]{:S(2)}) copy-start(f32[2308]{0:T(1024)} %copy-done.20) | copy-start | bytes 27700
  1102.4 69.4 %reduce-scatter.22.cloned.1.call-start = ((), (), s32[]{:S(2)}) async-start(), calls=%async_computation.15 | async-start | bytes 294912
  (28 other events, 289.2 us)
Sparse Core Ops, SparseCore 0:
  9.9 28.3 all-gather.6
  138.3 172.8 all-reduce.6
  313.1 26.7 all-gather.10
  341.6 28.0 all-gather.8
  390.9 211.1 all-reduce.8
  626.8 92.6 all-gather.12
  722.8 39.5 reduce-scatter.31
  765.6 41.0 reduce-scatter.19
  810.4 33.6 reduce-scatter.29
  847.0 34.0 reduce-scatter.27
  884.5 38.3 reduce-scatter.25
  925.6 172.6 all-reduce.10
  1102.5 32.6 reduce-scatter.23
  1138.1 33.6 reduce-scatter.21

commit v2 on v1

--- a/solution.py
+++ b/solution.py
@@ -536,197 +536,675 @@
     return ratio, mine(inputs), mine(cotangent), mask, small, w_qkv, w_out, w_up, w_down
 
 
-def normalize(tokens):
-    average = jnp.mean(tokens, axis=-1, keepdims=True)
-    centred = tokens - average
-    spread = jnp.mean(centred * centred, axis=-1, keepdims=True)
-    inverse = lax.rsqrt(spread + epsilon)
-    return (centred * inverse, inverse)
-
-
-def normalize_back(incoming, normed, inverse, gain):
-    scaled = incoming * gain
-    return inverse * (
-        scaled
-        - jnp.mean(scaled, axis=-1, keepdims=True)
-        - normed * jnp.mean(scaled * normed, axis=-1, keepdims=True)
+class Line:
+    def __init__(self, place, full, send, recv):
+        self.p, self.full, self.send, self.recv = place, full, send, recv
+
+    def up(self, src, o):
+        p = self.p
+        return remote(src, self.full.at[o], self.send.at[0, o], self.recv.at[o], p.dev(p.g, p.t + 1))
+
+    def down(self, src, o):
+        p = self.p
+        return remote(src, self.full.at[o], self.send.at[1, o], self.recv.at[o], p.dev(p.g, p.t - 1))
+
+    def pass_on(self, d, src=None):
+        p = self.p
+        t, last = p.t, p.length - 1
+
+        @pl.when(jnp.logical_and(t - d >= 0, t < last))
+        def _():
+            o = t - d
+            self.up(self.full.at[o] if src is None else src, o).start()
+
+        @pl.when(jnp.logical_and(t + d <= last, t > 0))
+        def _():
+            o = t + d
+            self.down(self.full.at[o] if src is None else src, o).start()
+
+    def arrive(self, d):
+        p = self.p
+        t, last = p.t, p.length - 1
+
+        @pl.when(t - d >= 0)
+        def _():
+            self.up(self.full.at[t - d], t - d).wait_recv()
+
+        @pl.when(t + d <= last)
+        def _():
+            self.down(self.full.at[t + d], t + d).wait_recv()
+
+    def drain(self, d, src=None):
+        p = self.p
+        t, last = p.t, p.length - 1
+
+        @pl.when(jnp.logical_and(t - d >= 0, t < last))
+        def _():
+            self.up(self.full.at[t - d] if src is None else src, t - d).wait_send()
+
+        @pl.when(jnp.logical_and(t + d <= last, t > 0))
+        def _():
+            self.down(self.full.at[t + d] if src is None else src, t + d).wait_send()
+
+
+def add_into(dst, src):
+    shape = dst.shape
+    n = shape[-2]
+    lead = 1
+    for s in shape[:-2]:
+        lead *= s
+    rows = min(n, 65536 // shape[-1])
+    per = n // rows
+
+    @pl.loop(0, lead * per)
+    def _(i):
+        r = pl.ds(aligned(lax.rem(i, per) * rows, rows), rows)
+        j = lax.div(i, per)
+        idx = []
+        for s in reversed(shape[:-2]):
+            idx.append(lax.rem(j, s))
+            j = lax.div(j, s)
+        idx = tuple(reversed(idx)) + (r, slice(None))
+        dst[idx] = dst[idx] + src[idx]
+
+
+class Scatter:
+    def __init__(self, place, index, kind, plane, bufs, out, sems):
+        self.p, self.a, self.kind, self.plane, self.out = place, index, kind, plane, out
+        self.ra, self.rb, self.xa, self.xb, self.below, self.above = bufs
+        self.send, self.recv = sems
+
+    def half(self, k, h):
+        n = self.plane.shape[-2] // 2
+        r = pl.ds(h * n, n)
+        if self.kind in ("o", "d"):
+            return self.plane.at[k, :, r, :]
+        if self.kind == "u":
+            return self.plane.at[:, k, r, :]
+        return self.plane.at[:, :, k, r, :]
+
+    def block(self, o):
+        k = self.k()
+        if self.kind in ("o", "d"):
+            return self.plane.at[k, o]
+        if self.kind == "u":
+            return self.plane.at[o, k]
+        return self.plane.at[:, o, k]
+
+    def k(self):
+        return self.p.y * 2 + self.p.x
+
+    def copy(self, slot, src, dst, dev):
+        return remote(src, dst, self.send.at[self.a, slot], self.recv.at[self.a, slot], dev)
+
+    def stage(self, slot):
+        p = self.p
+        ox, oy = 1 - p.x, 1 - p.y
+        to_x, to_y = p.dev(p.gx, p.t), p.dev(p.gy, p.t)
+        if slot == 0:
+            return self.copy(0, self.half(oy * 2 + ox, 0), self.ra.at[0], to_y)
+        if slot == 1:
+            return self.copy(1, self.half(oy * 2 + p.x, 0), self.ra.at[1], to_y)
+        if slot == 2:
+            return self.copy(2, self.half(oy * 2 + ox, 1), self.rb.at[0], to_x)
+        if slot == 3:
+            return self.copy(3, self.half(p.y * 2 + ox, 1), self.rb.at[1], to_x)
+        if slot == 4:
+            return self.copy(4, self.half(p.y * 2 + ox, 0), self.xa, to_x)
+        return self.copy(5, self.half(oy * 2 + p.x, 1), self.xb, to_y)
+
+    def first(self):
+        for slot in (0, 2, 1, 3):
+            self.stage(slot).start()
+
+    def cross(self):
+        p = self.p
+        ox, oy = 1 - p.x, 1 - p.y
+        self.stage(0).wait_recv()
+        add_into(self.half(p.y * 2 + ox, 0), self.ra.at[0])
+        self.stage(4).start()
+        yield
+        self.stage(2).wait_recv()
+        add_into(self.half(oy * 2 + p.x, 1), self.rb.at[0])
+        self.stage(5).start()
+        yield
+        self.stage(1).wait_recv()
+        add_into(self.half(self.k(), 0), self.ra.at[1])
+        yield
+        self.stage(3).wait_recv()
+        add_into(self.half(self.k(), 1), self.rb.at[1])
+        yield
+
+    def meet(self):
+        self.stage(4).wait_recv()
+        add_into(self.half(self.k(), 0), self.xa)
+        yield
+        self.stage(5).wait_recv()
+        add_into(self.half(self.k(), 1), self.xb)
+        yield
+
+    def up(self, o):
+        p = self.p
+        return self.copy(6 + o, self.block(o), self.below.at[o], p.dev(p.g, p.t + 1))
+
+    def down(self, o):
+        p = self.p
+        return self.copy(6 + p.length + o, self.block(o), self.above.at[o], p.dev(p.g, p.t - 1))
+
+    def line(self):
+        p = self.p
+        t, last = p.t, p.length - 1
+        for j in range(last):
+            o, q = last - j, j
+
+            @pl.when(o > t)
+            def _():
+                @pl.when(t > 0)
+                def _():
+                    self.up(o).wait_recv()
+                    add_into(self.block(o), self.below.at[o])
+
+                self.up(o).start()
+
+            @pl.when(q < t)
+            def _():
+                @pl.when(t < last)
+                def _():
+                    self.down(q).wait_recv()
+                    add_into(self.block(q), self.above.at[q])
+
+                self.down(q).start()
+
+            yield
+
+    def final(self, staged, sem):
+        p = self.p
+        t, last = p.t, p.length - 1
+
+        @pl.when(t > 0)
+        def _():
+            self.up(t).wait_recv()
+            add_into(self.block(t), self.below.at[t])
+
+        @pl.when(t < last)
+        def _():
+            self.down(t).wait_recv()
+            add_into(self.block(t), self.above.at[t])
+
+        c = pltpu.make_async_copy(self.block(t), self.out, sem)
+        c.start()
+        return c
+
+    def drain(self):
+        p = self.p
+        for slot in range(6):
+            self.stage(slot).wait_send()
+        for o in range(p.length):
+
+            @pl.when(jnp.logical_and(o > p.t, p.t < p.length - 1))
+            def _():
+                self.up(o).wait_send()
+
+            @pl.when(jnp.logical_and(o < p.t, p.t > 0))
+            def _():
+                self.down(o).wait_send()
+
+
+def scatter_buffers(kind, n, w, length):
+    half = {"q": (3, length, n // 2, w)}.get(kind, (length, n // 2, w))
+    full = {"q": (3, n, w)}.get(kind, (n, w))
+    return [pltpu.VMEM(s, bf16) for s in ((2,) + half, (2,) + half, half, half, (length,) + full, (length,) + full)]
+
+
+def load(src, dst, sem):
+    c = pltpu.make_async_copy(src, dst, sem)
+    c.start()
+    return c
+
+
+def mlp_back_kernel(ratio, length, vec_i, wd_i, wu_i, act_i, g_i, hid2_i, mid_i, ct_i, out_i,
+                    all_o, pd_o, pu_o, dmid_o, sums_o,
+                    vec, wd, wu, act, gg, hid2, mid, ct, acc, gds, gus, cd, cu, sums, red,
+                    line_s, line_r, core_s, core_r, ins, outs):
+    place = Place(ratio, length)
+    rows, width = ct.shape
+    nb = rows // 16
+    each = wu.shape[2]
+    enter(place, neighbours(place))
+    line = Line(place, all_o, line_s, line_r)
+    line.pass_on(0, out_i)
+    own = load(out_i, all_o.at[place.t], outs.at[0])
+    l_ct = load(ct_i, ct, ins.at[0])
+    l_wd = [load(wd_i.at[:, pl.ds(t * each, each), :], wd.at[:, pl.ds(t * each, each), :], ins.at[1 + t]) for t in range(length)]
+    l_g = load(g_i, gg, ins.at[5])
+    l_act = load(act_i, act, ins.at[6])
+    l_h = load(hid2_i, hid2, ins.at[7])
+    l_vec = load(vec_i, vec, ins.at[8])
+    l_wu = [load(wu_i.at[t], wu.at[t], ins.at[9 + t]) for t in range(length)]
+    l_mid = load(mid_i, mid, ins.at[13])
+    sums[...] = jnp.zeros_like(sums)
+    red[...] = jnp.zeros_like(red)
+    l_ct.wait()
+    l_g.wait()
+    other = 1 - place.core
+    writes = []
+
+    def sib(src, dst, a, t):
+        return remote(src, dst, core_s.at[a, t], core_r.at[a, t], place.dev(place.gs, place.t))
+
+    def to_d(t):
+        return sib(gds.at[t % 2, :, other], cd.at[:, t], 0, t)
+
+    def to_u(t):
+        return sib(gus.at[t % 2, :, other], cu.at[t], 1, t)
+
+    def settle(t):
+        to_d(t).wait_recv()
+        add_into(cd.at[:, t], gds.at[t % 2, :, place.core])
+        store_out(writes, cd.at[:, t], pd_o.at[:, t], outs.at[1 + t])
+        to_u(t).wait_recv()
+        add_into(cu.at[t], gus.at[t % 2, :, place.core])
+        store_out(writes, cu.at[t], pu_o.at[t], outs.at[5 + t])
+
+    for t in range(length):
+        cols = slice(t * each, (t + 1) * each)
+        l_wd[t].wait()
+        d = nt(ct[...], wide(wd, range(GROUPS), cols)) * gg[:, cols].astype(f32)
+        sums[8 + t : 9 + t, :] = jnp.sum(d, axis=0, keepdims=True)
+        gg[:, cols] = d.astype(bf16)
+        if t == 0:
+            l_act.wait()
+            l_h.wait()
+        if t >= 2:
+            to_d(t - 2).wait_send()
+            to_u(t - 2).wait_send()
+        down = tn(act[:, cols], ct[...]).astype(bf16)
+        for g in range(GROUPS):
+            gds[t % 2, g // 2, g % 2] = down[:, g * 128 : (g + 1) * 128]
+        to_d(t).start()
+        gus[t % 2] = tn(hid2[...], gg[:, cols]).astype(bf16).reshape(gus.shape[1:])
+        to_u(t).start()
+        if t > 0:
+            settle(t - 1)
+        l_wu[t].wait()
+        part = nt(gg[:, cols], wu[t])
+        if t == 0:
+            acc[...] = part
+        else:
+            acc[...] += part
+    settle(length - 1)
+    l_vec.wait()
+    l_mid.wait()
+    gain = vec[1:2, 0:width]
+
+    @pl.loop(0, nb)
+    def _(i):
+        r = pl.ds(aligned(i * 16, 16), 16)
+        n, inverse = statistics(mid[r, :])
+        dh = acc[r, :]
+        e = dh * gain
+        c = ct[r, :].astype(f32)
+        dm = c + inverse * (e - jnp.mean(e, axis=-1, keepdims=True) - n * jnp.mean(e * n, axis=-1, keepdims=True))
+        mid[r, :] = dm
+        for j, v in enumerate((dh * n, dh, dm, c)):
+            red[j] += v[0:8] + v[8:16]
+
+    for j, row in enumerate((1, 3, 4, 5)):
+        sums[row : row + 1, :] = jnp.sum(red[j], axis=0, keepdims=True)
+    store_out(writes, mid, dmid_o, outs.at[9])
+    store_out(writes, sums, sums_o, outs.at[10])
+    for t in (length - 2, length - 1):
+        to_d(t).wait_send()
+        to_u(t).wait_send()
+    line.arrive(1)
+    line.drain(0, out_i)
+    own.wait()
+    for c in writes:
+        c.wait()
+
+
+def mlp_back(ratio, length, vec, wd, wu, act, g, hid2, mid, ct, out):
+    rows, width = ct.shape
+    sds = jax.ShapeDtypeStruct
+    each = wu.shape[2]
+    n_u = wu.shape[1] // GROUPS
+    pd = ((GROUPS // 2, length, each, 128), bf16)
+    pu = ((length, GROUPS // 2, n_u, each), bf16)
+    sums = ((16, width), f32)
+    tok = ((rows, width), f32)
+    hid = ((rows, width), bf16)
+    scratch = [(vec.shape, f32), (wd.shape, bf16), (wu.shape, bf16), (act.shape, bf16), (act.shape, bf16), hid, tok, hid, tok,
+               ((2, GROUPS // 2, 2, each, 128), bf16), ((2, GROUPS // 2, 2, n_u, each), bf16), pd, pu, sums, ((4, 8, width), f32)]
+    dma = pltpu.SemaphoreType.DMA
+    outs = [((length, rows, width), bf16), pd, pu, tok, sums]
+    return pl.pallas_call(
+        functools.partial(mlp_back_kernel, ratio, length),
+        out_shape=[sds(*o) for o in outs],
+        in_specs=[any_spec()] * 9,
+        out_specs=[any_spec()] * len(outs),
+        scratch_shapes=[pltpu.VMEM(*s) for s in scratch]
+        + [dma((2, length)), dma((length,)), dma((2, length)), dma((2, length)), dma((14,)), dma((11,))],
+        compiler_params=pltpu.CompilerParams(collective_id=1, has_side_effects=True, vmem_limit_bytes=VMEM_LIMIT),
+        name="mlp_back",
+    )(vec, wd, wu, act, g, hid2, mid, ct, out)
+
+
+def attn_back_kernel(ratio, length, vec_i, wo_i, wq_i, hid1_i, qkv_i, att_i, lse_i, dmid_i, x_i, maskc_i, pd_i, pu_i, sums_i, all_i,
+                     all_o, gi_o, od_o, ou_o, oo_o, oq_o, sums_o,
+                     vec, wo, wq, hid1, qkv, att, lse, dmid, dmb, da, x, maskc, dh, gi, pd, pu, gos, gqs, co, cq, sums, got, red,
+                     *rest):
+    nbuf = 6
+    d_b, u_b, o_b, q_b = (rest[i * nbuf : (i + 1) * nbuf] for i in range(4))
+    rest = rest[4 * nbuf :]
+    line_s, line_r, gi_s, gi_r, core_s, core_r, sc_s, sc_r, sum_s, sum_r, ins, outs = rest
+    place = Place(ratio, length)
+    rows, width = dmid.shape
+    keys = qkv.shape[1]
+    nb = rows // 16
+    t = place.t
+    far = place.dev(place.g, t + 2 - 4 * lax.div(t, 2))
+    near = place.dev(place.g, t + 1 - 2 * lax.rem(t, 2))
+    enter(place, neighbours(place) + [(None, far)])
+    line = Line(place, all_o, line_s, line_r)
+    line.pass_on(1)
+    names = [(vec_i, vec), (pd_i, pd), (pu_i, pu), (dmid_i, dmid), (wo_i, wo), (att_i, att.at[pl.ds(0, rows)]), (lse_i, lse),
+             (qkv_i, qkv), (maskc_i, maskc), (wq_i, wq), (hid1_i, hid1), (x_i, x), (sums_i, sums.at[0])]
+    loads = [load(a, b, ins.at[i]) for i, (a, b) in enumerate(names)]
+    sd = Scatter(place, 0, "d", pd, d_b, od_o, (sc_s, sc_r))
+    su = Scatter(place, 1, "u", pu, u_b, ou_o, (sc_s, sc_r))
+    so = Scatter(place, 2, "o", co, o_b, oo_o, (sc_s, sc_r))
+    sq = Scatter(place, 3, "q", cq, q_b, oq_o, (sc_s, sc_r))
+    loads[1].wait()
+    sd.first()
+    loads[2].wait()
+    su.first()
+    for i in (0, 3, 4, 5, 6, 7, 8):
+        loads[i].wait()
+    other = 1 - place.core
+    writes = []
+    red[...] = jnp.zeros_like(red)
+    att[rows:keys, :] = jnp.zeros((keys - rows, width), bf16)
+    da[rows:keys, :] = jnp.zeros((keys - rows, width), bf16)
+    mlp = chain(sd.cross(), su.cross(), sd.meet(), sd.line(), su.meet(), su.line())
+
+    def sib(src, dst, a):
+        return remote(src, dst, core_s.at[a], core_r.at[a], place.dev(place.gs, t))
+
+    dmb[...] = dmid[...].astype(bf16)
+    da[0:rows, :] = nt(dmb[...], wide(wo, range(GROUPS))).astype(bf16)
+    g_out = tn(att[0:rows, :], dmb[...]).astype(bf16)
+    for g in range(GROUPS):
+        gos[g // 2, g % 2] = g_out[:, g * 128 : (g + 1) * 128].reshape(gos.shape[2:])
+    to_o = sib(gos.at[:, other], co, 0)
+    to_o.start()
+
+    pairs = width // 128
+    scale = HEAD ** (-0.5)
+
+    def back(p):
+        cols = pl.ds(aligned(p * 128, 128), 128)
+        k2 = qkv[1, :, cols]
+        v2 = qkv[2, :, cols]
+        low_k = lax.broadcasted_iota(jnp.int32, k2.shape, 1) < HEAD
+        dk = [None, None]
+        dv = [None, None]
+        total = jnp.zeros((1, 128), f32)
+        for r0, n in ((0, 256), (256, 256), (512, 128)):
+            q2 = qkv[0, r0 : r0 + n, cols]
+            da2 = da[r0 : r0 + n, cols]
+            prod = da2.astype(f32) * att[r0 : r0 + n, cols].astype(f32)
+            low = lax.broadcasted_iota(jnp.int32, (n, 128), 1) < HEAD
+            mc = jnp.concatenate([maskc[...]] * (n // 128), axis=1)
+            dq = []
+            for h in range(2):
+                mine = low if h == 0 else jnp.logical_not(low)
+                mine_k = low_k if h == 0 else jnp.logical_not(low_k)
+                delta = jnp.sum(jnp.where(mine, prod, 0.0), axis=-1, keepdims=True)
+                delta = jnp.concatenate(
+                    [jnp.transpose(jnp.broadcast_to(delta[i : i + 128], (128, 128)))[0:1, :] for i in range(0, n, 128)], axis=1
+                )
+                s = nt(jnp.where(mine_k, k2, jnp.zeros_like(k2)), q2)
+                prob = jnp.exp(s + mc - lse[p, h : h + 1, r0 : r0 + n])
+                dp = nt(jnp.where(mine_k, v2, jnp.zeros_like(v2)), da2)
+                ds = (prob * (dp - delta)).astype(bf16)
+                dq.append(tn(ds, k2))
+                a, b = nn(ds, q2), nn(prob.astype(bf16), da2)
+                dk[h] = a if dk[h] is None else dk[h] + a
+                dv[h] = b if dv[h] is None else dv[h] + b
+            d = jnp.where(low, dq[0], dq[1]) * scale
+            total = total + jnp.sum(d, axis=0, keepdims=True)
+            qkv[0, r0 : r0 + n, cols] = d.astype(bf16)
+        v = jnp.where(low_k, dv[0], dv[1])
+        qkv[1, :, cols] = jnp.where(low_k, dk[0], dk[1]).astype(bf16)
+        qkv[2, :, cols] = v.astype(bf16)
+        red[2, 0:1, cols] = total
+        red[2, 1:2, cols] = jnp.sum(v, axis=0, keepdims=True)
+
+    for part in range(pairs):
+
+        @pl.loop(0, 1)
+        def _(j):
+            back(part + j)
+
+        if part in (3, 5, 6):
+            step(mlp, 2)
+        if part == 4:
+            to_o.wait_recv()
+            add_into(co, gos.at[:, place.core])
+            so.first()
+
+    loads[9].wait()
+    for c in range(3):
+        part = nt(qkv[c, 0:rows, :], wide(wq.at[c], range(length)))
+        if c == 0:
+            dh[...] = part
+        else:
+            dh[...] += part
+    loads[11].wait()
+    gain = vec[0:1, 0:width]
+
+    @pl.loop(0, nb)
+    def _(i):
+        r = pl.ds(aligned(i * 16, 16), 16)
+        n, inverse = statistics(x[r, :].astype(f32))
+        d = dh[r, :]
+        e = d * gain
+        gi[r, :] = (
+            dmid[r, :] + inverse * (e - jnp.mean(e, axis=-1, keepdims=True) - n * jnp.mean(e * n, axis=-1, keepdims=True))
+        ).astype(bf16)
+        for j, v in enumerate((d * n, d)):
+            red[j] += v[0:8] + v[8:16]
+
+    gline = Line(place, gi_o, gi_s, gi_r)
+    gline.pass_on(0, gi)
+    own = load(gi, gi_o.at[t], outs.at[0])
+    loads[12].wait()
+    sums[0, 0:1, :] = jnp.sum(red[0], axis=0, keepdims=True)
+    sums[0, 2:3, :] = jnp.sum(red[1], axis=0, keepdims=True)
+    sums[0, 6:8, :] = red[2, 0:2, :]
+
+    loads[10].wait()
+    to_q = []
+    for c in range(3):
+        g_c = tn(hid1[...], qkv[c, 0:rows, :]).astype(bf16)
+        for o in range(length):
+            w = gqs.shape[-1]
+            gqs[c, o] = g_c[:, o * w : (o + 1) * w].reshape(gqs.shape[2:])
+        q = sib(gqs.at[c, :, :, other], cq.at[c], 1 + c)
+        q.start()
+        to_q.append(q)
+        step(mlp, 2)
+    for c in range(3):
+        to_q[c].wait_recv()
+        add_into(cq.at[c], gqs.at[c, :, :, place.core])
+    sq.first()
+
+    partners = [place.dev(place.gs, t), place.dev(place.gx, t), place.dev(place.gy, t), near, far]
+    pair = [remote(sums.at[i], got.at[i], sum_s.at[i], sum_r.at[i], dev) for i, dev in enumerate(partners)]
+
+    def add_sums(i):
+        pair[i].wait_recv()
+        sums[i + 1] = sums[i] + got[i]
+        if i + 1 < len(pair):
+            pair[i + 1].start()
+
+    line.arrive(2)
+    line.pass_on(2)
+    pair[0].start()
+    tail = chain(so.cross(), so.meet(), so.line())
+    for i in range(len(pair)):
+        step(mlp)
+        add_sums(i)
+    for _ in range(10):
+        step(mlp)
+        step(tail)
+    for _ in mlp:
+        pass
+    for _ in tail:
+        pass
+    store_out(writes, sums.at[len(pair)], sums_o, outs.at[5])
+    writes.append(sd.final(None, outs.at[1]))
+    writes.append(su.final(None, outs.at[2]))
+    for _ in chain(sq.cross(), sq.meet()):
+        pass
+    line.arrive(3)
+    gline.arrive(1)
+    gline.pass_on(1)
+    for _ in sq.line():
+        pass
+    writes.append(so.final(None, outs.at[3]))
+    writes.append(sq.final(None, outs.at[4]))
+    gline.arrive(2)
+    gline.pass_on(2)
+    gline.arrive(3)
+    for s in (sd, su, so, sq):
+        s.drain()
+    to_o.wait_send()
+    for q in to_q + pair:
+        q.wait_send()
+    line.drain(1)
+    line.drain(2)
+    gline.drain(0, gi)
+    gline.drain(1)
+    gline.drain(2)
+    own.wait()
+    for c in writes:
+        c.wait()
+
+
+def attn_back(ratio, length, vec, wo, wq, hid1, qkv, att, lse, dmid, x, maskc, pd, pu, sums, out_all):
+    rows, width = x.shape
+    keys = qkv.shape[1]
+    sds = jax.ShapeDtypeStruct
+    each = pu.shape[3]
+    n_o, n_q, w_q = wo.shape[1] // length, wq.shape[2] // GROUPS, wq.shape[3]
+    n_u, n_d = pu.shape[2], pd.shape[2]
+    half = GROUPS // 2
+    hid, tok = ((rows, width), bf16), ((rows, width), f32)
+    tall = ((keys, width), bf16)
+    outs = [(out_all.shape, bf16), (out_all.shape, bf16), ((n_d, 128), bf16), ((n_u, each), bf16), ((n_o, 128), bf16),
+            ((3, n_q, w_q), bf16), (sums.shape, f32)]
+    scratch = [(vec.shape, f32), (wo.shape, bf16), (wq.shape, bf16), hid, (qkv.shape, bf16), tall, (lse.shape, f32), tok, hid, tall, hid,
+               (maskc.shape, f32), tok, hid, (pd.shape, bf16), (pu.shape, bf16),
+               ((half, 2, length, n_o, 128), bf16), ((3, length, half, 2, n_q, w_q), bf16),
+               ((half, length, n_o, 128), bf16), ((3, length, half, n_q, w_q), bf16),
+               ((6,) + sums.shape, f32), ((5,) + sums.shape, f32), ((3, 8, width), f32)]
+    bufs = (scatter_buffers("d", n_d, 128, length) + scatter_buffers("u", n_u, each, length)
+            + scatter_buffers("o", n_o, 128, length) + scatter_buffers("q", n_q, w_q, length))
+    dma = pltpu.SemaphoreType.DMA
+    return pl.pallas_call(
+        functools.partial(attn_back_kernel, ratio, length),
+        out_shape=[sds(*o) for o in outs],
+        in_specs=[any_spec()] * 14,
+        out_specs=[any_spec()] * len(outs),
+        scratch_shapes=[pltpu.VMEM(*s) for s in scratch] + bufs
+        + [dma((2, length)), dma((length,)), dma((2, length)), dma((length,)), dma((4,)), dma((4,)),
+           dma((4, 6 + 2 * length)), dma((4, 6 + 2 * length)), dma((5,)), dma((5,)), dma((13,)), dma((6,))],
+        input_output_aliases={13: 0},
+        compiler_params=pltpu.CompilerParams(collective_id=2, has_side_effects=True, vmem_limit_bytes=VMEM_LIMIT),
+        name="attn_back",
+    )(vec, wo, wq, hid1, qkv, att, lse, dmid, x, maskc, pd, pu, sums, out_all)
+
+
+def place_kernel(out_i, gi_i, out_o, gi_o, buf_a, buf_b):
+    length, rows, width = out_i.shape
+    lanes = width // 128
+    for r0 in range(0, rows, 16):
+        base = r0 * lanes * length
+        for b in range(length):
+            a = out_i[b, r0 : r0 + 16, :].astype(f32)
+            g = gi_i[b, r0 : r0 + 16, :].astype(f32)
+            for j in range(lanes):
+                at = pl.ds(base + j * length + b, 16, stride=lanes * length)
+                buf_a[at, :] = a[:, j * 128 : (j + 1) * 128]
+                gi_o[at, :] = g[:, j * 128 : (j + 1) * 128]
+    out_o[...] = buf_a[...].astype(bf16)
+
+
+def place_out(out_all, gi_all, seq):
+    length, rows, width = out_all.shape
+    lanes = width // 128
+    blk = 64
+    flat = seq * lanes * length
+    spec_i = pl.BlockSpec((length, blk, width), lambda i: (0, i, 0))
+    spec_o = pl.BlockSpec((blk * lanes * length, 128), lambda i: (i, 0))
+    out, gi = pl.pallas_call(
+        place_kernel,
+        grid=(-(-seq // blk),),
+        out_shape=[jax.ShapeDtypeStruct((flat, 128), bf16), jax.ShapeDtypeStruct((flat, 128), f32)],
+        in_specs=[spec_i, spec_i],
+        out_specs=[spec_o, spec_o],
+        scratch_shapes=[pltpu.VMEM((blk * lanes * length, 128), f32), pltpu.VMEM((8, 128), f32)],
+        name="place_out",
+    )(out_all, gi_all)
+
+    def shape(a):
+        return a.reshape(seq, lanes, length, 128).transpose(2, 0, 1, 3).reshape(length, seq, width)
+
+    return shape(out), shape(gi)
+
+
+def local(inputs, lengths, norm_gains, norm_shifts, w_qkv, bias_qv, w_out, out_bias, w_up, b_up, w_down, cotangent):
+    length = lax.axis_size("tensor")
+    fsdp = lax.axis_size("fsdp")
+    seq = inputs.shape[1]
+    ratio, x, ct, mask, small, q_s, o_s, u_s, d_s = prepare(
+        length, inputs, lengths, norm_gains, norm_shifts, w_qkv, bias_qv, w_out, out_bias, w_up, b_up, w_down, cotangent, fsdp
     )
-
-
-def masked_scores(query_heads, key_heads, valid, scale):
-    scores = (
-        jnp.einsum("bqhe,bkhe->bhqk", query_heads, key_heads, preferred_element_type=jnp.float32)
-        * scale
+    vec, wq, wo, wu, wd, hid1, qkv, att, lse, mid, hid2, act, gate, out = forward(
+        ratio, length, x, mask[None, :], small, q_s, o_s, u_s, d_s
     )
-    return jnp.where(valid[:, None, None, :], scores, -jnp.inf)
-
-
-def local(
-    inputs,
-    lengths,
-    norm_gains,
-    norm_shifts,
-    w_qkv,
-    bias_qv,
-    w_out,
-    out_bias,
-    w_up,
-    b_up,
-    w_down,
-    cotangent,
-):
-    batch, seq_len, width = inputs.shape
-    tokens = batch * seq_len
-    local_width = w_qkv.shape[2]
-    local_heads = local_width // HEAD
-    scale = HEAD ** (-0.5)
-    gathered = (
-        lax.all_gather(w_qkv, "fsdp", axis=1, tiled=True),
-        lax.all_gather(w_out, "fsdp", axis=1, tiled=True),
-        lax.all_gather(w_up, "fsdp", axis=0, tiled=True),
-        lax.all_gather(w_down, "fsdp", axis=1, tiled=True),
-        lax.all_gather(norm_gains, "fsdp", axis=1, tiled=True),
-        lax.all_gather(norm_shifts, "fsdp", axis=1, tiled=True),
-        lax.all_gather(out_bias, "fsdp", axis=1, tiled=True),
+    out_all, pd, pu, dmid, sums = mlp_back(ratio, length, vec, wd, wu, act, gate, hid2, mid, ct, out)
+    maskc = jnp.broadcast_to(mask[:, None], (mask.shape[0], 128))
+    out_all, gi_all, od, ou, oo, oq, sums = attn_back(
+        ratio, length, vec, wo, wq, hid1, qkv, att, lse, dmid, x, maskc, pd, pu, sums, out_all
     )
-    full_qkv, full_out, full_up, full_down, all_gains, all_shifts, all_bias = gathered
-    gain_rows = all_gains.astype(jnp.float32)
-    shift_rows = all_shifts.astype(jnp.float32)
-    bias_rows = all_bias.astype(jnp.float32)
-    proj_bias = bias_qv.astype(jnp.float32)
-    hidden_bias = b_up.astype(jnp.float32)
-    flat_in = inputs.reshape(tokens, width).astype(jnp.float32)
-    normed_one, inverse_one = normalize(flat_in)
-    hidden_one = (normed_one * gain_rows[0] + shift_rows[0]).astype(jnp.bfloat16)
-    projected = jnp.einsum("rd,cde->cre", hidden_one, full_qkv, preferred_element_type=jnp.float32)
-    queries = (projected[0] + proj_bias[0]).astype(jnp.bfloat16)
-    key_rows = projected[1].astype(jnp.bfloat16)
-    value_rows = (projected[2] + proj_bias[1]).astype(jnp.bfloat16)
-    head_shape = (batch, seq_len, local_heads, HEAD)
-    query_heads = queries.reshape(head_shape)
-    key_heads = key_rows.reshape(head_shape)
-    value_heads = value_rows.reshape(head_shape)
-    valid = lax.broadcasted_iota(jnp.int32, (batch, seq_len), 1) < lengths[:, None]
-    scores = masked_scores(query_heads, key_heads, valid, scale)
-    top = jnp.max(scores, axis=-1, keepdims=True)
-    log_total = top + jnp.log(jnp.sum(jnp.exp(scores - top), axis=-1, keepdims=True))
-    weights_b = jnp.exp(scores - log_total).astype(jnp.bfloat16)
-    attended_heads = jnp.einsum(
-        "bhqk,bkhe->bqhe", weights_b, value_heads, preferred_element_type=jnp.float32
-    ).astype(jnp.bfloat16)
-    attended = attended_heads.reshape(tokens, local_width)
-    attn_total = lax.psum(
-        jnp.dot(attended, full_out, preferred_element_type=jnp.float32).astype(jnp.bfloat16),
-        "tensor",
-    ).astype(jnp.float32)
-    middle = flat_in + (attn_total + bias_rows[0])
-    normed_two, inverse_two = normalize(middle)
-    hidden_two = (normed_two * gain_rows[1] + shift_rows[1]).astype(jnp.bfloat16)
-    before = jnp.dot(hidden_two, full_up, preferred_element_type=jnp.float32) + hidden_bias
-    activated = jax.nn.gelu(before, approximate=False).astype(jnp.bfloat16)
-    mlp_total = lax.psum(
-        jnp.dot(activated, full_down, preferred_element_type=jnp.float32).astype(jnp.bfloat16),
-        "tensor",
-    ).astype(jnp.float32)
-    ratio, x_own, _ct, mask, small, q_s, o_s, u_s, d_s = prepare(
-        w_qkv.shape[2] and lax.axis_size("tensor"), inputs, lengths, norm_gains, norm_shifts, w_qkv, bias_qv, w_out, out_bias,
-        w_up, b_up, w_down, cotangent, lax.axis_size("fsdp"))
-    own = forward(ratio, lax.axis_size("tensor"), x_own, mask[None, :], small, q_s, o_s, u_s, d_s)[-1]
-    result = lax.all_gather(own[:seq_len], "tensor", axis=0)
-    back_qkv, back_out, back_up, back_down = (full_qkv, full_out, full_up, full_down)
-    grad_rows = cotangent.reshape(tokens, width)
-    grad_f = grad_rows.astype(jnp.float32)
-    grad_down = jnp.einsum("rf,rd->fd", activated, grad_rows, preferred_element_type=jnp.float32)
-    dact = jnp.einsum("rd,fd->rf", grad_rows, back_down, preferred_element_type=jnp.float32)
-    normal_cdf = 0.5 * (1.0 + jax.scipy.special.erf(before * half_root))
-    density = jnp.exp(-0.5 * before * before) * density_scale
-    dbefore = dact * (normal_cdf + before * density)
-    dbefore_b = dbefore.astype(jnp.bfloat16)
-    grad_b_up = jnp.sum(dbefore, axis=0)
-    grad_up = jnp.einsum("rd,rf->df", hidden_two, dbefore_b, preferred_element_type=jnp.float32)
-    dhidden_two = lax.psum(
-        jnp.einsum("rf,df->rd", dbefore_b, back_up, preferred_element_type=jnp.float32).astype(
-            jnp.bfloat16
-        ),
-        "tensor",
-    ).astype(jnp.float32)
-    dmiddle = grad_f + normalize_back(dhidden_two, normed_two, inverse_two, gain_rows[1])
-    dmiddle_b = dmiddle.astype(jnp.bfloat16)
-    grad_out = jnp.einsum("rk,rd->kd", attended, dmiddle_b, preferred_element_type=jnp.float32)
-    grad_out_bias = jnp.stack([jnp.sum(dmiddle, axis=0), jnp.sum(grad_f, axis=0)])
-    dattended = jnp.einsum(
-        "rd,kd->rk", dmiddle_b, back_out, preferred_element_type=jnp.float32
-    ).astype(jnp.bfloat16)
-    dattended_heads = dattended.reshape(head_shape)
-    again_scores = masked_scores(query_heads, key_heads, valid, scale)
-    prob = jnp.exp(again_scores - log_total)
-    again_weights = prob.astype(jnp.bfloat16)
-    dprob = jnp.einsum(
-        "bqhe,bkhe->bhqk", dattended_heads, value_heads, preferred_element_type=jnp.float32
-    )
-    delta = jnp.einsum(
-        "bqhe,bqhe->bhq", dattended_heads, attended_heads, preferred_element_type=jnp.float32
-    )[..., None]
-    dscores = (prob * (dprob - delta) * scale).astype(jnp.bfloat16)
-    dqueries = jnp.einsum(
-        "bhqk,bkhe->bqhe", dscores, key_heads, preferred_element_type=jnp.float32
-    ).reshape(tokens, local_width)
-    dkeys = jnp.einsum(
-        "bhqk,bqhe->bkhe", dscores, query_heads, preferred_element_type=jnp.float32
-    ).reshape(tokens, local_width)
-    dvalues = jnp.einsum(
-        "bhqk,bqhe->bkhe", again_weights, dattended_heads, preferred_element_type=jnp.float32
-    ).reshape(tokens, local_width)
-    grad_bias_part = jnp.stack([jnp.sum(dqueries, axis=0), jnp.sum(dvalues, axis=0)])
-    stacked = jnp.stack([dqueries, dkeys, dvalues]).astype(jnp.bfloat16)
-    grad_qkv = jnp.einsum("rd,cre->cde", hidden_one, stacked, preferred_element_type=jnp.float32)
-    dhidden_one = lax.psum(
-        jnp.einsum("cre,cde->rd", stacked, back_qkv, preferred_element_type=jnp.float32).astype(
-            jnp.bfloat16
-        ),
-        "tensor",
-    ).astype(jnp.float32)
-    grad_input = dmiddle + normalize_back(dhidden_one, normed_one, inverse_one, gain_rows[0])
-    grad_gains = jnp.stack(
-        [jnp.sum(dhidden_one * normed_one, axis=0), jnp.sum(dhidden_two * normed_two, axis=0)]
-    )
-    grad_shifts = jnp.stack([jnp.sum(dhidden_one, axis=0), jnp.sum(dhidden_two, axis=0)])
-    owned_qkv, owned_out, owned_up, owned_down, owned_gains, owned_shifts, owned_bias = (
-        lax.psum_scatter(
-            grad_qkv.astype(jnp.bfloat16), "fsdp", scatter_dimension=1, tiled=True
-        ).astype(jnp.float32),
-        lax.psum_scatter(
-            grad_out.astype(jnp.bfloat16), "fsdp", scatter_dimension=1, tiled=True
-        ).astype(jnp.float32),
-        lax.psum_scatter(
-            grad_up.astype(jnp.bfloat16), "fsdp", scatter_dimension=0, tiled=True
-        ).astype(jnp.float32),
-        lax.psum_scatter(
-            grad_down.astype(jnp.bfloat16), "fsdp", scatter_dimension=1, tiled=True
-        ).astype(jnp.float32),
-        lax.psum_scatter(
-            grad_gains.astype(jnp.bfloat16), "fsdp", scatter_dimension=1, tiled=True
-        ).astype(jnp.float32),
-        lax.psum_scatter(
-            grad_shifts.astype(jnp.bfloat16), "fsdp", scatter_dimension=1, tiled=True
-        ).astype(jnp.float32),
-        lax.psum_scatter(
-            grad_out_bias.astype(jnp.bfloat16), "fsdp", scatter_dimension=1, tiled=True
-        ).astype(jnp.float32),
-    )
-    summed_bias_qv, summed_b_up = lax.psum((grad_bias_part, grad_b_up), "fsdp")
+    output, grad_input = place_out(out_all, gi_all, seq)
+    if ratio > 1:
+        groups = [[g * ratio + r for r in range(ratio)] for g in range(GROUPS)]
+        across = [[g * ratio + r for g in range(GROUPS)] for r in range(ratio)]
+
+        def cut(a, axis):
+            return lax.psum_scatter(a, "fsdp", scatter_dimension=axis, tiled=True, axis_index_groups=groups)
+
+        od, ou, oo, oq = cut(od, 1), cut(ou, 0), cut(oo, 1), cut(oq, 1)
+        sums = lax.psum(sums, "fsdp", axis_index_groups=groups)
+    width = inputs.shape[2]
+    f, t = lax.axis_index("fsdp"), lax.axis_index("tensor")
+    own = lax.dynamic_slice_in_dim(sums[0:6], f * (width // fsdp), width // fsdp, 1)
+    heads = width // length
     return (
-        result.reshape(batch, seq_len, width),
-        grad_input.reshape(batch, seq_len, width),
-        owned_gains,
-        owned_shifts,
-        owned_qkv,
-        summed_bias_qv,
-        owned_out,
-        owned_bias,
-        owned_up,
-        summed_b_up,
-        owned_down,
+        output,
+        grad_input,
+        own[0:2],
+        own[2:4],
+        oq.astype(f32),
+        lax.dynamic_slice_in_dim(sums[6:8], t * heads, heads, 1),
+        oo.astype(f32),
+        own[4:6],
+        ou.astype(f32),
+        lax.dynamic_index_in_dim(sums, 8 + t, 0, keepdims=False),
+        od.astype(f32),
     )
 
 

time: 1190 us -> 461 us (0.39)
  waiting for transfers between devices: 470 us -> 0 us
  Pallas kernels: 224 us -> 430 us
  matrix products: 171 us -> 0 us
  local copies, waits for them, and re-layouts: 148 us -> 18.9 us
  other arithmetic: 101 us -> 4.99 us
  blocking collectives: 49.6 us -> 0 us
  between operations: 15.1 us -> 1.25 us
    psum x3 -> x0, waiting for transfers between devices: 324 us -> none  [the longest x1 173 us: local(): lax.psum(jnp.einsum('cre,cde->rd', stacked, back_qkv, preferred_element_t...]
    pallas_call x0 -> x3, Pallas kernels: none -> 277 us  [the longest x1 214 us: attn_back(): pl.pallas_call(functools.partial(attn_back_kernel, ratio, length), out_sh...]
    dot_general x17 -> x0, matrix products: 171 us -> none  [the longest x1 27.9 us: local(): jnp.einsum('rf,rd->fd', activated, grad_rows, preferred_element_type=jnp....]
    unnamed x20 -> x0, waiting for transfers between devices: 117 us -> none
    reduce_sum x13 -> x0, other arithmetic: 73.5 us -> none  [the longest x2 14.1 us: normalize(): average = jnp.mean(tokens, axis=-1, keepdims=True)]
    pallas_call x1, Pallas kernels: 224 us -> 153 us  [forward(): pl.pallas_call(functools.partial(forward_kernel, ratio, length), out_shap...]
    unnamed x100 -> x24, local copies, waits for them, and re-layouts: 58.6 us -> 2.59 us
    all_gather x4 -> x0, blocking collectives: 36.9 us -> none  [the longest x1 10.2 us: local(): lax.all_gather(norm_gains, 'fsdp', axis=1, tiled=True)]
  transfers between devices with their start and end apart: 14 -> 0, of which waited for: 8 -> 0; matrix products, arithmetic and copies ran while one was open for 27% -> 0% of each run, Pallas kernels for 19% -> 0%
where the time goes in v2:
time: 461 us; the launch traced here: 455 us
  Pallas kernels  430 us (93%)
  local copies, waits for them, and re-layouts  18.9 us (4%)
  other arithmetic  4.99 us (1%)
    pallas_call x1, Pallas kernels, attn_back(): pl.pallas_call(functools.partial(attn_back_kernel, ratio, length), out_sh...  214 us
    pallas_call x1, Pallas kernels, forward(): pl.pallas_call(functools.partial(forward_kernel, ratio, length), out_shap...  153 us
    pallas_call x1, Pallas kernels, mlp_back(): pl.pallas_call(functools.partial(mlp_back_kernel, ratio, length), out_sha...  46.6 us
    pallas_call x1, Pallas kernels, place_out(): pl.pallas_call(place_kernel, grid=(-(-seq // blk),), out_shape=[jax.Shape...  16.7 us
    dynamic_slice x1, local copies, waits for them, and re-layouts, mine(): a = lax.dynamic_index_in_dim(a, t, 0, keepdims=False)  10.1 us

profile of v2, /device:TPU:0, one launch (start us, length us, event | category | flops | bytes accessed | tf_op | source)
XLA Modules:
  0.0 455.3 jit_solution(4611577481940924726)
XLA Ops:
  0.6 10.1 %constant_dynamic-slice_fusion.3 = (bf16[1,577,1024]{2,0,1:T(2,128)(2,1)}, bf16[1,577,1024]{2,0,1:T(2,128)(2,1)S(1)}) fusion(bf16[4,577,1024]{2,0,1:T(4,128)(2,1)} %param.23, s32[]{:T(128)S(6)} %select_n.34, bf16[4,577,1024]{2,0,1:T(4,128)(2,1)} %param.12), kind=kLoop, calls=%fused_computation.8 | loop fusion | bytes 4726788 | tf_op jit(solution)/shard_map/jit(dynamic_index_in_dim)/dynamic_slice | solution.py:527
  10.7 0.0 copy-start.8
  10.7 0.0 copy-start.9
  10.7 0.4 copy.35
  11.2 1.1 pad.11.x.x_i
  12.3 0.6 dynamic_slice.22
  12.9 1.2 compare_select_fusion.mask
  14.2 0.2 concatenate.3
  14.4 0.6 pad.12.s_s
  15.0 152.8 %forward.1 = (f32[16,4096]{1,0:T(8,128)}, bf16[3,4,1024,256]{3,2,1,0:T(8,128)(2,1)}, bf16[8,1024,128]{2,1,0:T(8,128)(2,1)}, bf16[4,1024,1024]{2,1,0:T(8,128)(2,1...) custom-call(bf16[592,1024]{1,0:T(8,128)(2,1)} %pad.11.x.x_i, ...), custom_call_target="tpu_custom_call" | custom-call | tf_op jit(solution)/shard_map/forward/pallas_call | solution.py:500
  167.8 2.1 copy.34
  169.9 1.1 pad.13.ct_i
  171.0 46.6 %mlp_back.1 = (bf16[4,592,1024]{2,1,0:T(8,128)(2,1)}, bf16[4,4,1024,128]{3,2,1,0:T(8,128)(2,1)}, bf16[4,4,128,1024]{3,2,1,0:T(8,128)(2,1)}, f32[592,1024]{1,0:T(8,128)}, f32[16,1024]{1,0:T(8,128)}) custom-call(f32[16,4096]{1,0:T(8,128)} %get-tuple-element.39.vec_i, bf16[8,4096,128]{2,1,0:T(8,128)(2,1)} %get-tuple-element.46.wd_i, ...), custom_call_target="tpu_custom_call" | custom-call | tf_op jit(solution)/shard_map/mlp_back/pallas_call | solution.py:880
  217.6 0.7 fusion
  218.2 0.9 broadcast_in_dim.23.maskc_i
  219.1 214.2 %attn_back.1 = (bf16[4,592,1024]{2,1,0:T(8,128)(2,1)}, bf16[4,592,1024]{2,1,0:T(8,128)(2,1)}, bf16[1024,128]{1,0:T(8,128)(2,1)}, bf16[128,1024]{1,0:T(8,128)(2,1...) custom-call(f32[16,4096]{1,0:T(8,128)} %get-tuple-element.39.vec_i, ...), custom_call_target="tpu_custom_call", output_to_operand_aliasing={{0}: (13, {})} | custom-call | tf_op jit(solution)/shard_map/attn_back/pallas_call | solution.py:1115
  433.3 16.7 %place_out.1 = (bf16[18464,128]{1,0:T(8,128)(2,1)}, f32[18464,128]{1,0:T(8,128)}) custom-call(bf16[4,592,1024]{2,1,0:T(8,128)(2,1)} %get-tuple-element.58.out_i, bf16[4,592,1024]{2,1,0:T(8,128)(2,1)} %get-tuple-element.59.gi_i), custom_call_target="tpu_custom_call" | custom-call | tf_op jit(solution)/shard_map/place_out/pallas_call | solution.py:1151
  450.0 0.6 fusion.1
  450.6 0.8 convert_element_type.17
  451.4 0.6 constant_dynamic-slice_fusion.1
  452.0 0.7 convert_element_type.18
  452.6 0.8 convert_element_type.19
  453.5 0.6 constant_dynamic-slice_fusion
  454.1 0.8 convert_element_type.20
  (24 shorter events, 0.1 us)
Async XLA Ops:
  10.7 1.6 copy-start.10
  10.7 3.4 copy-start.6
  10.7 3.4 copy-start.5
  10.7 3.4 copy-start.7
  10.7 3.4 copy-start.8
  10.7 3.4 copy-start.9
  433.3 16.7 %copy-start.4 = (f32[16,1024]{1,0:T(8,128)S(1)}, f32[16,1024]{1,0:T(8,128)}, u32[]{:S(2)}) copy-start(f32[16,1024]{1,0:T(8,128)} %get-tuple-element.62) | copy-start | bytes 196612
  433.3 17.3 %copy-start.2 = (bf16[3,128,256]{2,1,0:T(8,128)(2,1)S(1)}, bf16[3,128,256]{2,1,0:T(8,128)(2,1)}, u32[]{:S(2)}) copy-start(bf16[3,128,256]{2,1,0:T(8,128)(2,1)} %get-tuple-element.63) | copy-start | bytes 589828
  433.3 18.7 %copy-start.3 = (bf16[256,128]{1,0:T(8,128)(2,1)S(1)}, bf16[256,128]{1,0:T(8,128)(2,1)}, u32[]{:S(2)}) copy-start(bf16[256,128]{1,0:T(8,128)(2,1)} %get-tuple-element.64) | copy-start | bytes 196612
  433.3 19.3 %copy-start.1 = (bf16[128,1024]{1,0:T(8,128)(2,1)S(1)}, bf16[128,1024]{1,0:T(8,128)(2,1)}, u32[]{:S(2)}) copy-start(bf16[128,1024]{1,0:T(8,128)(2,1)} %get-tuple-element.65) | copy-start | bytes 786436
  433.3 20.7 %copy-start = (bf16[1024,128]{1,0:T(8,128)(2,1)S(1)}, bf16[1024,128]{1,0:T(8,128)(2,1)}, u32[]{:S(2)}) copy-start(bf16[1024,128]{1,0:T(8,128)(2,1)} %get-tuple-element.66) | copy-start | bytes 786436
